TPU v7x, 512 devices: a whole 4x8x8 slice. The times are simulated.
512 devices in a mesh: obs: 32 (over x, y), det: 16 (over z, core).
Axes of the slice: x: 4, y: 8, z: 8, core: 2. Of those that a mesh axis runs over, the one named last changes fastest.
Arguments:
- sky: bfloat16 [1024, 3, 16, 128], P('obs'), may hold values from -6 to 6
- tile_list: int32 [32, 32], replicated, may hold values from 0 to 1023, as said below
- along: bfloat16 [32, 32, 128, 128], P('obs'), may hold values from -0.5 to 0.5
- detector_kernel: bfloat16 [1536, 48], P('det'), may hold values from -0.875 to 0.875
- sample_weight: bfloat16 [1536, 131072], P('det', 'obs'), may hold values from 0 to 2
- noise_inverse: bfloat16 [16, 1536, 1536], P('det', 'obs'), may hold values from -8 to 8, as said below
Outputs:
- normal_sky: float32 [1024, 3, 16, 128], P('obs')
Inputs may be any that keep to these rules, and one draw needn't show every extreme that they name: `tile_list`: row p lists 32 different tiles; tile n is owned by index n // 32 of obs; a row holds at most 2 tiles of one owner, and every row holds exactly 2 tiles of some owner. `noise_inverse`: each band's matrix is symmetric.
All inputs are finite; a program needn't handle non-finite values.
Results may differ from a plain program's by a relative error of at most 0.0042.
Values may be sent and summed in bfloat16 or wider, within the bound.
A program may use at most 64 MiB of HBM per device.

v0:
```python
import math

import jax
import jax.numpy as jnp
from jax import lax
from jax.sharding import PartitionSpec as P

SLOW = 16
FAST = 256
ROWS = 16
COLS = 128
CAP = 2


def dft_tables():
    slow_index = jnp.arange(SLOW, dtype=jnp.int32)
    fast_index = jnp.arange(FAST, dtype=jnp.int32)
    slow_angle = (
        2.0
        * math.pi
        / SLOW
        * (slow_index[:, None] * slow_index[None, :] % SLOW).astype(jnp.float32)
    )
    fast_angle = (
        2.0
        * math.pi
        / FAST
        * (fast_index[:, None] * fast_index[None, :] % FAST).astype(jnp.float32)
    )
    twist_angle = (
        2.0
        * math.pi
        / (SLOW * FAST)
        * (slow_index[:, None] * fast_index[None, :] % (SLOW * FAST)).astype(jnp.float32)
    )
    slow_scale = 1.0 / math.sqrt(SLOW)
    fast_scale = 1.0 / math.sqrt(FAST)
    return (
        (jnp.cos(slow_angle) * slow_scale).astype(jnp.bfloat16),
        (jnp.sin(slow_angle) * slow_scale).astype(jnp.bfloat16),
        (jnp.cos(fast_angle) * fast_scale).astype(jnp.bfloat16),
        (jnp.sin(fast_angle) * fast_scale).astype(jnp.bfloat16),
        jnp.cos(twist_angle),
        jnp.sin(twist_angle),
    )


def product(pattern, left_side, right_side):
    return jnp.einsum(pattern, left_side, right_side, preferred_element_type=jnp.float32)


def forward_transform(signal, tables):
    slow_cos, slow_sin, fast_cos, fast_sin, twist_cos, twist_sin = tables
    first_real = product("gv,nvu->ngu", slow_cos, signal)
    first_imag = -product("gv,nvu->ngu", slow_sin, signal)
    half_real = (first_real * twist_cos + first_imag * twist_sin).astype(jnp.bfloat16)
    half_imag = (first_imag * twist_cos - first_real * twist_sin).astype(jnp.bfloat16)
    spec_real = product("fu,ngu->ngf", fast_cos, half_real) + product(
        "fu,ngu->ngf", fast_sin, half_imag
    )
    spec_imag = product("fu,ngu->ngf", fast_cos, half_imag) - product(
        "fu,ngu->ngf", fast_sin, half_real
    )
    return (spec_real.astype(jnp.bfloat16), spec_imag.astype(jnp.bfloat16))


def inverse_transform(mix_real, mix_imag, tables):
    slow_cos, slow_sin, fast_cos, fast_sin, twist_cos, twist_sin = tables
    back_real = product("fu,ngf->ngu", fast_cos, mix_real) - product(
        "fu,ngf->ngu", fast_sin, mix_imag
    )
    back_imag = product("fu,ngf->ngu", fast_cos, mix_imag) + product(
        "fu,ngf->ngu", fast_sin, mix_real
    )
    turn_real = (back_real * twist_cos - back_imag * twist_sin).astype(jnp.bfloat16)
    turn_imag = (back_imag * twist_cos + back_real * twist_sin).astype(jnp.bfloat16)
    return product("gv,ngu->nvu", slow_cos, turn_real) - product("gv,ngu->nvu", slow_sin, turn_imag)


def local(sky, tile_list, along, detector_kernel, sample_weight, noise_inverse):
    tables = dft_tables()
    blocks = lax.axis_size("obs")
    my_block = lax.axis_index("obs")
    tile_dev = sky.shape[0]
    listed = tile_list.shape[1]
    local_dets = detector_kernel.shape[0]
    all_dets = noise_inverse.shape[2]
    owner_all = tile_list // tile_dev
    positions = jnp.arange(listed)
    same_owner = owner_all[:, :, None] == owner_all[:, None, :]
    earlier = positions[None, :] < positions[:, None]
    rank_all = jnp.sum((same_owner & earlier[None]).astype(jnp.int32), axis=2)
    owned_here = owner_all == my_block
    local_all = tile_list - my_block * tile_dev
    slot_hit = (
        owned_here[:, :, None] & (rank_all[:, :, None] == jnp.arange(CAP)[None, None, :])
    ).astype(jnp.float32)
    local_hit = (local_all[:, :, None] == jnp.arange(tile_dev)[None, None, :]).astype(jnp.float32)
    owner_pick = jnp.einsum("pjc,pjl->pcl", slot_hit, local_hit).reshape(blocks * CAP, tile_dev)
    my_owner = lax.dynamic_index_in_dim(owner_all, my_block, 0, keepdims=False)
    my_rank = lax.dynamic_index_in_dim(rank_all, my_block, 0, keepdims=False)
    recv_index = my_owner * CAP + my_rank
    send_pick = (recv_index[None, :] == jnp.arange(blocks * CAP)[:, None]).astype(jnp.float32)
    sky_flat = sky.reshape(tile_dev, -1)
    outgoing = jnp.dot(
        owner_pick.astype(jnp.bfloat16), sky_flat, preferred_element_type=jnp.float32
    )
    outgoing = outgoing.astype(jnp.bfloat16).reshape(blocks, CAP, 3, ROWS, COLS)
    received = lax.all_to_all(outgoing, "obs", split_axis=0, concat_axis=0, tiled=True)
    fetched = received.reshape(blocks * CAP, 3 * ROWS, COLS)[recv_index]
    block_along = along[0]
    scan_rows = (
        product("kmc,kcu->mku", fetched, block_along).astype(jnp.bfloat16).reshape(3 * ROWS, -1)
    )
    weight_wide = sample_weight.astype(jnp.float32)
    timestream = (
        jnp.dot(detector_kernel, scan_rows, preferred_element_type=jnp.float32) * weight_wide
    ).astype(jnp.bfloat16)
    spec_real, spec_imag = forward_transform(timestream.reshape(local_dets, SLOW, FAST), tables)
    spectra = jnp.stack([spec_real, spec_imag], axis=1)
    banded = lax.all_to_all(spectra, "det", split_axis=3, concat_axis=0, tiled=True)
    band_cols = banded.shape[3]
    columns = banded.reshape(all_dets, 2 * SLOW * band_cols)
    mixed_cols = jnp.dot(
        lax.all_gather(noise_inverse, "obs", axis=1, tiled=True)[0],
        columns,
        preferred_element_type=jnp.float32,
    )
    mixed = mixed_cols.astype(jnp.bfloat16).reshape(all_dets, 2, SLOW, band_cols)
    returned = lax.all_to_all(mixed, "det", split_axis=0, concat_axis=3, tiled=True)
    restored = inverse_transform(returned[:, 0], returned[:, 1], tables)
    filtered = (restored.reshape(local_dets, -1) * weight_wide).astype(jnp.bfloat16)
    projected = product(
        "dku,kcu->dkc", filtered.reshape(local_dets, listed, -1), block_along
    ).astype(jnp.bfloat16)
    tile_terms = product("dkc,dm->kmc", projected, detector_kernel)
    summed = lax.psum(tile_terms, "det")
    outgoing_sums = jnp.dot(
        send_pick,
        summed.reshape(listed, -1),
        precision=lax.Precision.HIGHEST,
        preferred_element_type=jnp.float32,
    )
    incoming = lax.all_to_all(
        outgoing_sums.reshape(blocks, CAP, 3 * ROWS * COLS),
        "obs",
        split_axis=0,
        concat_axis=0,
        tiled=True,
    )
    normal = lax.dot_general(
        owner_pick,
        incoming.reshape(blocks * CAP, -1),
        (((0,), (0,)), ((), ())),
        precision=lax.Precision.HIGHEST,
        preferred_element_type=jnp.float32,
    )
    normal = normal.reshape(tile_dev, 3, ROWS, COLS)
    return normal


def solution(mesh):
    in_specs = (
        P("obs", None, None, None),
        P(),
        P("obs", None, None, None),
        P("det", None),
        P("det", "obs"),
        P("det", "obs", None),
    )
    out_specs = P("obs", None, None, None)
    return jax.shard_map(local, mesh=mesh, in_specs=in_specs, out_specs=out_specs, check_vma=False)
```

profile of v0, /device:TPU:1, one launch (start us, length us, event | category | flops | bytes accessed | tf_op | source)
XLA Modules:
  0.0 428.0 jit_solution(466994780856783526)
XLA Ops:
  6.5 0.7 all-gather.2.cloned.1.call-update
  7.3 0.7 broadcast_compare_fusion
  8.0 0.8 convert_reduce_fusion
  8.8 0.7 broadcast_subtract_fusion
  9.8 1.3 fusion.18
  11.2 1.0 copy.98
  12.2 10.5 %all-to-all-start = ((bf16[32,2,3,16,128]{4,3,2,1,0:T(8,128)(2,1)}), bf16[32,2,3,16,128]{4,3,2,1,0:T(8,128)(2,1)S(1)}, u32[]{:S(2)}, u32[]{:S(2)}) async-start(bf16[32,2,3,16,128]{4,3,2,1,0:T(8,128)(2,1)} %bitcast.50), calls=%async_computation | async-start | bytes 1572864 | tf_op jit(solution)/shard_map/all_to_all | solution.py:109
  22.9 20.2 %all-to-all-done = bf16[32,2,3,16,128]{4,3,2,1,0:T(8,128)(2,1)S(1)} async-done(((bf16[32,2,3,16,128]{4,3,2,1,0:T(8,128)(2,1)}), bf16[32,2,3,16,128]{4,3,2,1,0:T(8,128)(2,1)S(1)}, u32[]{:S(2)}, u32[]{:S(2)}) %all-to-all-start) | async-done | bytes 786464 | tf_op jit(solution)/shard_map/all_to_all | solution.py:109
  43.1 0.6 gather_fusion
  43.7 0.4 fusion.19
  44.2 0.4 fusion.3
  44.8 0.5 fusion.93
  45.2 0.7 fusion.9
  45.9 1.3 fusion.61
  47.3 1.3 fusion.17
  48.6 1.3 fusion.63
  49.9 1.3 fusion.16
  51.2 1.3 pad_maximum_fusion
  52.5 4.0 copy.71
  56.5 68.2 %all_to_all.43 = bf16[96,2,16,256]{0,2,1,3:T(8,128)(2,1)S(1)} all-to-all(bf16[96,2,16,256]{0,2,1,3:T(8,128)(2,1)S(1)} %copy.71), channel_id=1, replica_groups=mesh['obs'=32,'det'=16] {'det'}, dimensions={3} | all-to-all | bytes 3145728 | tf_op jit(solution)/shard_map/all_to_all | solution.py:121
  124.7 1.4 copy.73
  126.1 3.4 reshape.150
  129.5 5.4 %fusion.4 = bf16[512,1536]{1,0:T(8,128)(2,1)S(1)} fusion(bf16[1536,512]{0,1:T(8,128)(2,1)} %reshape.150, bf16[1,1536,1536]{2,1,0:T(8,128)(2,1)} %all-gather.2.cloned.1.call-done), kind=kOutput, calls=%fused_computation.7 | convolution fusion | flops 2416705536 | bytes 7864320 | tf_op jit(solution)/shard_map/dot_general | solution.py:124
  134.9 17.4 %copy.74 = bf16[1536,2,16,16]{3,2,1,0:T(8,128)(2,1)} copy(bf16[1536,2,16,16]{0,3,2,1:T(8,128)(2,1)S(1)} %bitcast.172) | data formatting | bytes 3145728 | tf_op jit(solution)/shard_map/reshape | solution.py:129
  152.3 16.7 %reshape.173 = bf16[16,2,24576]{2,1,0:T(2,128)(2,1)S(1)} reshape(bf16[1536,2,16,16]{3,2,1,0:T(8,128)(2,1)} %copy.74) | data formatting | bytes 3145728
  169.0 42.6 %all_to_all.44 = bf16[16,2,24576]{2,1,0:T(2,128)(2,1)} all-to-all(bf16[16,2,24576]{2,1,0:T(2,128)(2,1)S(1)} %reshape.173), channel_id=1, replica_groups=mesh['obs'=32,'det'=16] {'det'}, dimensions={0} | all-to-all | bytes 3145728 | tf_op jit(solution)/shard_map/all_to_all | solution.py:130
  211.6 14.5 %reshape.174 = bf16[1536,2,16,16]{3,2,1,0:T(8,128)(2,1)} reshape(bf16[16,2,24576]{2,1,0:T(2,128)(2,1)} %all_to_all.44) | data formatting | bytes 3145728
  226.1 12.6 %copy.76 = bf16[96,2,16,16,16]{0,4,3,2,1:T(8,128)(2,1)S(1)} copy(bf16[96,2,16,16,16]{4,2,1,0,3:T(8,128)(2,1)} %bitcast.159) | data formatting | bytes 3145728 | tf_op jit(solution)/shard_map/all_to_all | solution.py:130
  238.7 1.5 fusion.156
  240.2 1.7 copy.94
  241.9 2.5 fusion.31
  244.4 1.7 copy.93
  246.1 1.3 fusion.35
  247.5 1.3 convolution_add_fusion
  248.8 1.3 convolution_subtract_fusion
  250.2 0.4 fusion.23
  250.6 0.5 convolution_subtract_fusion.1
  251.1 1.1 copy.100
  252.2 2.1 fusion.15
  254.3 1.1 copy.119
  255.5 109.8 %all-reduce.2.cloned.1.call-done = f32[32,6144]{1,0:T(8,128)} async-done(((f32[32,6144]{1,0:T(8,128)}), f32[32,6144]{1,0:T(8,128)}) %all-reduce.2.cloned.1.call-update) | async-done | bytes 786448 | tf_op jit(solution)/shard_map/psum | solution.py:137
  365.3 2.0 fusion.29
  367.2 1.2 copy.80
  368.5 46.1 %all_to_all.45 = f32[32,2,6144]{2,1,0:T(2,128)S(1)} all-to-all(f32[32,2,6144]{2,1,0:T(2,128)S(1)} %copy.80), channel_id=1, replica_groups=mesh['obs'=32,'det'=16] {'obs'}, dimensions={0} | all-to-all | bytes 3145728 | tf_op jit(solution)/shard_map/all_to_all | solution.py:144
  414.5 2.2 reshape.155
  416.8 1.7 copy.102
  418.5 1.4 fusion.12
  419.9 1.3 copy.83
  (18 shorter events, 0.8 us)
Async XLA Ops:
  6.5 37.2 %copy-start = (bf16[1,32,128,128]{3,2,1,0:T(8,128)(2,1)S(1)}, bf16[1,32,128,128]{3,2,1,0:T(8,128)(2,1)}, u32[]{:S(2)}) copy-start(bf16[1,32,128,128]{3,2,1,0:T(8,128)(2,1)} %param.8) | copy-start | bytes 3145732
  6.5 122.9 %all-gather.2.cloned.1.call-start = ((), (), s32[]{:S(2)}) async-start(), calls=%async_computation.4 | async-start | bytes 4866048 | tf_op jit(solution)/shard_map/all_gather | solution.py:125
  12.2 30.9 %all-to-all-start = ((bf16[32,2,3,16,128]{4,3,2,1,0:T(8,128)(2,1)}), bf16[32,2,3,16,128]{4,3,2,1,0:T(8,128)(2,1)S(1)}, u32[]{:S(2)}, u32[]{:S(2)}) async-start(bf16[32,2,3,16,128]{4,3,2,1,0:T(8,128)(2,1)} %bitcast.50), calls=%async_computation | async-start | bytes 1572864 | tf_op jit(solution)/shard_map/all_to_all | solution.py:109
  22.7 21.5 %copy-start.2 = (bf16[96,4096]{1,0:T(8,128)(2,1)S(1)}, bf16[96,4096]{1,0:T(8,128)(2,1)}, u32[]{:S(2)}) copy-start(bf16[96,4096]{1,0:T(8,128)(2,1)} %param.10) | copy-start | bytes 2359300
  22.7 21.5 %copy-start.3 = (bf16[96,48]{0,1:T(8,128)(2,1)S(1)}, bf16[96,48]{0,1:T(8,128)(2,1)}, u32[]{:S(2)}) copy-start(bf16[96,48]{0,1:T(8,128)(2,1)} %param.9) | copy-start | bytes 27652
  22.7 342.6 %all-reduce.2.cloned.1.call-start = ((), (), s32[]{:S(2)}) async-start(), calls=%async_computation.5 | async-start | bytes 1572864 | tf_op jit(solution)/shard_map/psum | solution.py:137
  246.1 1.4 copy-start.1
Sparse Core Ops, SparseCore 0:
  10.5 92.3 all-gather.1
  255.6 109.6 all-reduce.1
where the time goes:
time: 433 us; the launch traced here: 428 us
  blocking collectives  157 us (36%)
  waiting for transfers between devices  131 us (30%)
  local copies, waits for them, and re-layouts  85.4 us (20%)
  matrix products  27.1 us (6%)
  between operations  13.7 us (3%)
  starting transfers between devices  10.5 us (2%)
    psum x1, waiting for transfers between devices, local(): summed = lax.psum(tile_terms, 'det')  110 us
    all_to_all x1, blocking collectives, local(): lax.all_to_all(spectra, 'det', split_axis=3, concat_axis=0, tiled=True)  68.2 us
    all_to_all x1, blocking collectives, local(): lax.all_to_all(outgoing_sums.reshape(blocks, CAP, 3 * ROWS * COLS), 'obs'...  46.1 us
    all_to_all x1, blocking collectives, local(): lax.all_to_all(mixed, 'det', split_axis=0, concat_axis=3, tiled=True)  42.6 us
    unnamed x17, local copies, waits for them, and re-layouts  39.8 us
    all_to_all x1, waiting for transfers between devices, local(): lax.all_to_all(outgoing, 'obs', split_axis=0, concat_axis=0, tiled=True)  20.2 us
    reshape x1, local copies, waits for them, and re-layouts, local(): mixed_cols.astype(jnp.bfloat16).reshape(all_dets, 2, SLOW, band_cols)  17.4 us
    dot_general x14, matrix products, product(): jnp.einsum(pattern, left_side, right_side, preferred_element_type=jnp.flo...  16.3 us
  transfers between devices with their start and end apart: 3, of which 2 were waited for; matrix products, arithmetic and copies ran while one was open for 5% of the time, Pallas kernels for 0%

commit v1 on v0

v1 whole, which is shorter than its diff:
```python
import functools
import math

import jax
import jax.numpy as jnp
import numpy as np
from jax import lax
from jax.experimental import pallas as pl
from jax.experimental.pallas import tpu as pltpu
from jax.sharding import PartitionSpec as P

CAP = 2
MP = 4
FAST = 256
LANES = 128
MESH = pl.DeviceIdType.MESH
F32 = jnp.float32
BF16 = jnp.bfloat16
VMEM = pl.BlockSpec(memory_space=pltpu.VMEM)


def tables(slow):
    lane = np.arange(FAST)
    half, rest = lane // LANES, lane % LANES
    j, i = rest // slow, rest % slow
    w = half * LANES + i * (LANES // slow) + j
    r = np.arange(FAST)
    angle = 2 * np.pi / FAST * (w[:, None] * r[None, :] % FAST)
    c, s = np.cos(angle) / math.sqrt(FAST), np.sin(angle) / math.sqrt(FAST)
    forward = np.concatenate([c, -s], 1)
    inverse = np.concatenate([c.T, -s.T], 0)
    twist = 2 * np.pi / (slow * FAST) * (np.arange(slow)[:, None] * r[None, :])
    tw = np.stack([np.cos(twist), np.sin(twist)], 1) / math.sqrt(slow)
    return (
        jnp.asarray(forward, BF16),
        jnp.asarray(inverse, BF16),
        jnp.asarray(tw.reshape(slow, 2, FAST), F32),
    )


def small_dft(re, im, sign):
    n = len(re)
    if n == 1:
        return re, im
    er, ei = small_dft(re[0::2], im[0::2], sign)
    odr, odi = small_dft(re[1::2], im[1::2], sign)
    outr, outi = [None] * n, [None] * n
    for k in range(n // 2):
        if k == 0:
            tr, ti = odr[0], odi[0]
        elif 4 * k == n:
            tr, ti = (-odi[k], odr[k]) if sign > 0 else (odi[k], -odr[k])
        else:
            c = math.cos(2 * math.pi * k / n)
            s = sign * math.sin(2 * math.pi * k / n)
            if 8 * k == n:
                tr, ti = (
                    c * (odr[k] - sign * odi[k]),
                    c * (odi[k] + sign * odr[k]),
                )
            else:
                tr, ti = c * odr[k] - s * odi[k], c * odi[k] + s * odr[k]
        outr[k], outi[k] = er[k] + tr, ei[k] + ti
        outr[k + n // 2], outi[k + n // 2] = er[k] - tr, ei[k] - ti
    return outr, outi


def digit_swap(tiles):
    n = len(tiles)
    tiles = list(tiles)
    lane = lax.broadcasted_iota(jnp.int32, tiles[0].shape, 1)
    step = 1
    while step < n:
        odd = (lane // step) % 2 == 1
        for i in range(n):
            if i & step:
                continue
            a, b = tiles[i], tiles[i | step]
            tiles[i] = jnp.where(odd, pltpu.roll(b, step, 1), a)
            tiles[i | step] = jnp.where(odd, b, pltpu.roll(a, LANES - step, 1))
        step *= 2
    return tiles


def greet(obs, det, with_obs, det_peers):
    barrier = pltpu.get_barrier_semaphore()
    count = 0
    if with_obs:
        me = lax.axis_index("obs")

        def signal(d, carry):
            pl.semaphore_signal(
                barrier, inc=1, device_id={"obs": lax.rem(me + d, obs)}, device_id_type=MESH
            )
            return carry

        lax.fori_loop(1, obs, signal, 0)
        count += obs - 1
    for peer in det_peers:
        pl.semaphore_signal(barrier, inc=1, device_id={"det": peer}, device_id_type=MESH)
    count += len(det_peers)
    pl.semaphore_wait(barrier, count)


def same_core(det):
    me = lax.axis_index("det")
    others = [lax.rem(me + 2 * d, det) for d in range(1, det // 2)]
    partner = me + 1 - 2 * lax.rem(me, 2)
    return others, partner


def obs_exchange(obs, src, dst, send_sem, recv_sem):
    me = lax.axis_index("obs")

    def copy(d):
        to = lax.rem(me + d, obs)
        return pltpu.make_async_remote_copy(
            src_ref=src.at[to],
            dst_ref=dst.at[me],
            send_sem=send_sem.at[d],
            recv_sem=recv_sem.at[d],
            device_id={"obs": to},
            device_id_type=MESH,
        )

    def start(d, carry):
        copy(d).start()
        return carry

    def wait(d, carry):
        copy(d).wait()
        return carry

    lax.fori_loop(1, obs, start, 0)
    dst[me] = src[me]
    lax.fori_loop(1, obs, wait, 0)


def det_gather(det, full, sems):
    send_sem, recv_sem, pass_send, pass_recv = sems
    me = lax.axis_index("det")
    others, partner = same_core(det)

    def copy(slot, to, a, b):
        return pltpu.make_async_remote_copy(
            src_ref=full.at[slot],
            dst_ref=full.at[slot],
            send_sem=a,
            recv_sem=b,
            device_id={"det": to},
            device_id_type=MESH,
        )

    n = det // 2
    order = sorted(range(1, n), key=lambda d: -min(d, n - d))
    outs = []
    for d in order:
        outs.append(copy(me, others[d - 1], send_sem.at[d], recv_sem.at[d]))
        outs[-1].start()
    outs.append(copy(me, partner, pass_send.at[0], pass_recv.at[0]))
    outs[-1].start()
    for d in reversed(order):
        source = lax.rem(me + det - 2 * d, det)
        copy(source, me, send_sem.at[d], recv_sem.at[d]).wait_recv()
        outs.append(copy(source, partner, pass_send.at[d], pass_recv.at[d]))
        outs[-1].start()
    for d in range(n):
        source = lax.rem(partner + det - 2 * d, det)
        copy(source, partner, pass_send.at[d], pass_recv.at[d]).wait_recv()
    for out in outs:
        out.wait_send()


def pair_products(rows, along, k, transposed):
    dims = (((1,), (1 if transposed else 0,)), ((), ()))
    first = lax.dot_general(rows, along[k], dims, preferred_element_type=F32)
    second = lax.dot_general(rows, along[k + 1], dims, preferred_element_type=F32)
    index = lax.broadcasted_iota(jnp.int32, first.shape, 0)
    return jnp.where(index < MP, first, second)


def split_dot(exact, x, dims):
    high = x.astype(BF16)
    low = (x - high.astype(F32)).astype(BF16)
    dot = functools.partial(lax.dot_general, dimension_numbers=dims, preferred_element_type=F32)
    return dot(exact, high) + dot(exact, low)


ROWS_COLS = (((1,), (0,)), ((), ()))
COLS_COLS = (((0,), (0,)), ((), ()))


def fetch_kernel(obs, det, out_ref, pick_ref, along_ref, scan_ref, recv, fetched, s0, s1, *sems):
    others, partner = same_core(det)
    greet(obs, det, True, others + [partner])
    obs_exchange(obs, out_ref, recv, s0, s1)
    flat = recv[...].reshape(obs * CAP * MP, LANES).astype(BF16)
    fetched[...] = jnp.dot(pick_ref[...], flat, preferred_element_type=F32).astype(BF16)
    me = lax.axis_index("det")
    tiles = along_ref.shape[0]
    for k in range(0, tiles, 4):
        rows = fetched[4 * k : 4 * k + 16]
        low = pair_products(rows[:8], along_ref, k, False)
        high = pair_products(rows[8:], along_ref, k + 2, False)
        scan_ref[me, 4 * k : 4 * k + 16] = jnp.concatenate([low, high], 0).astype(BF16)
    det_gather(det, scan_ref, sems)


def forward_kernel(slow, ke_ref, scan_ref, w_ref, fwd_ref, tw_ref, x_ref, ts, u, half):
    dets = w_ref.shape[0]
    tiles = w_ref.shape[1] // LANES
    for i in range(tiles // 4):
        rhs = scan_ref[:, 16 * i : 16 * i + 16, :].reshape(slow * 16, LANES)
        rows = jnp.dot(ke_ref[...], rhs, preferred_element_type=F32)
        for q in range(4):
            k = 4 * i + q
            ts[k] = rows[q * dets : (q + 1) * dets] * w_ref[:, k * LANES : (k + 1) * LANES].astype(F32)

    for h in range(2):

        def swap(g, carry):
            at = pl.ds(pl.multiple_of(g * 16, 16), 16)
            out = digit_swap([ts[h * slow + i, at, :] for i in range(slow)])
            for z in range(slow):
                u[z, at, h * LANES : (h + 1) * LANES] = out[z].astype(BF16)
            return carry

        lax.fori_loop(0, dets // 16, swap, 0)

    def fast(z, carry):
        a = jnp.dot(u[z], fwd_ref[...], preferred_element_type=F32)
        re, im = a[:, :FAST], a[:, FAST:]
        c, s = tw_ref[z, 0:1, :], tw_ref[z, 1:2, :]
        half[z, :, :FAST] = re * c + im * s
        half[z, :, FAST:] = im * c - re * s
        return carry

    lax.fori_loop(0, slow, fast, 0)

    for rc in range(2):
        lo, hi = rc * LANES, FAST + rc * LANES

        def last(g, carry):
            at = pl.ds(pl.multiple_of(g * 16, 16), 16)
            re = [half[z, at, lo : lo + LANES] for z in range(slow)]
            im = [half[z, at, hi : hi + LANES] for z in range(slow)]
            re, im = small_dft(re, im, -1)
            for b in range(slow):
                x_ref[b, at, lo : lo + LANES] = re[b].astype(BF16)
                x_ref[b, at, hi : hi + LANES] = im[b].astype(BF16)
            return carry

        lax.fori_loop(0, dets // 16, last, 0)


def inverse_kernel(slow, y_ref, w_ref, ke_ref, inv_ref, tw_ref, g_ref, turned, ts):
    dets = w_ref.shape[0]
    tiles = w_ref.shape[1] // LANES
    for rc in range(2):
        lo, hi = rc * LANES, FAST + rc * LANES

        def first(g, carry):
            at = pl.ds(pl.multiple_of(g * 16, 16), 16)
            re = [y_ref[b, at, lo : lo + LANES].astype(F32) for b in range(slow)]
            im = [y_ref[b, at, hi : hi + LANES].astype(F32) for b in range(slow)]
            re, im = small_dft(re, im, 1)
            for z in range(slow):
                c, s = tw_ref[z, 0:1, lo : lo + LANES], tw_ref[z, 1:2, lo : lo + LANES]
                turned[z, at, lo : lo + LANES] = (re[z] * c - im[z] * s).astype(BF16)
                turned[z, at, hi : hi + LANES] = (im[z] * c + re[z] * s).astype(BF16)
            return carry

        lax.fori_loop(0, dets // 16, first, 0)

    def fast(z, carry):
        o = jnp.dot(turned[z], inv_ref[...], preferred_element_type=F32)
        ts[z] = o[:, :LANES]
        ts[slow + z] = o[:, LANES:]
        return carry

    lax.fori_loop(0, slow, fast, 0)

    for h in range(2):

        def swap(g, carry):
            at = pl.ds(pl.multiple_of(g * 16, 16), 16)
            out = digit_swap([ts[h * slow + z, at, :] for z in range(slow)])
            for i in range(slow):
                ts[h * slow + i, at, :] = out[i]
            return carry

        lax.fori_loop(0, dets // 16, swap, 0)

    for i in range(tiles // 4):
        filtered = [
            (ts[k] * w_ref[:, k * LANES : (k + 1) * LANES].astype(F32)).astype(BF16)
            for k in range(4 * i, 4 * i + 4)
        ]
        rows = lax.dot_general(
            ke_ref[...], jnp.concatenate(filtered, 0), COLS_COLS, preferred_element_type=F32
        )
        g_ref[:, 16 * i : 16 * i + 16, :] = rows.reshape(slow, 16, LANES).astype(BF16)


def all_det(det):
    me = lax.axis_index("det")
    return [lax.rem(me + d, det) for d in range(1, det)]


def spread_kernel(det, x_ref, out_ref, send_sem, recv_sem):
    me = lax.axis_index("det")
    peers = all_det(det)
    greet(0, det, False, peers)
    copies = []
    for d in sorted(range(1, det), key=lambda d: -min(d, det - d)):
        copies.append(
            pltpu.make_async_remote_copy(
                src_ref=x_ref.at[peers[d - 1]],
                dst_ref=out_ref.at[me],
                send_sem=send_sem.at[d],
                recv_sem=recv_sem.at[d],
                device_id={"det": peers[d - 1]},
                device_id_type=MESH,
            )
        )
        copies[-1].start()
    out_ref[me] = x_ref[me]
    for copy in copies:
        copy.wait()


def mix_kernel(det, dets, n_ref, x_ref, out_ref, staged, send_sem, recv_sem):
    me = lax.axis_index("det")
    peers = all_det(det) + [me]
    greet(0, det, False, peers[:-1])
    copies = []
    for s in range(0, det, 4):
        rows = [
            n_ref[pl.ds(pl.multiple_of(to * dets, 16), dets), :] for to in peers[s : s + 4]
        ]
        got = jnp.dot(jnp.concatenate(rows, 0), x_ref[...], preferred_element_type=F32)
        got = got.astype(BF16)
        for i in range(4):
            d = s + i + 1
            block = got[i * dets : (i + 1) * dets]
            if d == det:
                out_ref[me] = block
                continue
            staged[d - 1] = block
            copies.append(
                pltpu.make_async_remote_copy(
                    src_ref=staged.at[d - 1],
                    dst_ref=out_ref.at[me],
                    send_sem=send_sem.at[d],
                    recv_sem=recv_sem.at[d],
                    device_id={"det": peers[d - 1]},
                    device_id_type=MESH,
                )
            )
            copies[-1].start()
    for copy in copies:
        copy.wait()


def give_kernel(
    obs, det, g_ref, along_ref, pick_ref, own_ref, sel_ref, sky_ref,
    parts, sums, terms, leave, recv, full, r0, r1, s0, s1, *sems,
):
    me = lax.axis_index("det")
    peers = all_det(det)
    greet(obs, det, True, peers)
    copies = []
    for d in sorted(range(1, det), key=lambda d: -min(d, det - d)):
        copies.append(
            pltpu.make_async_remote_copy(
                src_ref=g_ref.at[peers[d - 1]],
                dst_ref=parts.at[me],
                send_sem=r0.at[d],
                recv_sem=r1.at[d],
                device_id={"det": peers[d - 1]},
                device_id_type=MESH,
            )
        )
        copies[-1].start()
    parts[me] = g_ref[me]
    for copy in copies:
        copy.wait()
    total = parts[0].astype(F32)
    for j in range(1, det):
        total = total + parts[j].astype(F32)
    sums[...] = total
    tiles = along_ref.shape[0]
    for k in range(0, tiles, 2):
        rows = sums[4 * k : 4 * k + 8]
        high = rows.astype(BF16)
        low = (rows - high.astype(F32)).astype(BF16)
        terms[4 * k : 4 * k + 8] = pair_products(high, along_ref, k, True) + pair_products(
            low, along_ref, k, True
        )
    out = split_dot(pick_ref[...], terms[...], COLS_COLS)
    leave[...] = out.reshape(obs, CAP * MP, LANES)
    obs_exchange(obs, leave, recv, s0, s1)
    flat = recv[...].reshape(obs * CAP * MP, LANES)
    full[me] = split_dot(own_ref[...], flat, COLS_COLS).astype(BF16)
    det_gather(det, full, sems)
    held = sky_ref.shape[0]
    rows_all = sky_ref.shape[1]
    for i in range(held // 4):
        rhs = full[:, 16 * i : 16 * i + 16, :].reshape(det * 16, LANES)
        got = jnp.dot(sel_ref[...], rhs, preferred_element_type=F32)
        sky_ref[4 * i : 4 * i + 4] = got.reshape(4, rows_all, LANES)


def call(kernel, out, scratch, name, collective=None):
    if collective is None:
        params = pltpu.CompilerParams(vmem_limit_bytes=56 * 2**20)
    else:
        params = pltpu.CompilerParams(
            vmem_limit_bytes=56 * 2**20, collective_id=collective, has_side_effects=True
        )

    def run(*args):
        return pl.pallas_call(
            kernel,
            out_shape=out,
            in_specs=[VMEM] * len(args),
            out_specs=VMEM,
            scratch_shapes=scratch,
            compiler_params=params,
            name=name,
        )(*args)

    return run


def dma(n):
    return [pltpu.SemaphoreType.DMA((n,))] * 2


def local(sky, tile_list, along, detector_kernel, sample_weight, noise_inverse):
    obs, det = lax.axis_size("obs"), lax.axis_size("det")
    me_obs, me_det = lax.axis_index("obs"), lax.axis_index("det")
    held, tiles = sky.shape[0], tile_list.shape[1]
    dets, all_dets = detector_kernel.shape[0], noise_inverse.shape[2]
    rows_all = sky.shape[1] * sky.shape[2]
    mine = rows_all // det
    fwd, inv, tw = tables(det)

    noise = lax.all_gather(noise_inverse, "obs", axis=1, tiled=True)[0]

    owner = tile_list // held
    earlier = jnp.arange(tiles)[None, :] < jnp.arange(tiles)[:, None]
    rank = jnp.sum(
        ((owner[:, :, None] == owner[:, None, :]) & earlier[None]).astype(jnp.int32), axis=2
    )
    slot_hit = (
        (owner == me_obs)[:, None, :] & (rank[:, None, :] == jnp.arange(CAP)[None, :, None])
    )
    inside = tile_list - me_obs * held
    wanted = jnp.max(jnp.where(slot_hit, inside[:, None, :] + 1, 0), axis=2) - 1
    wanted = jnp.broadcast_to(wanted[:, :, None], (obs, CAP, MP))
    row = jnp.arange(MP)[None, None, :]
    wanted = jnp.where(wanted >= 0, wanted * MP + row, -1).reshape(obs * CAP * MP, 1)
    own = (wanted == jnp.arange(held * MP)[None, :]).astype(BF16)
    slot = lax.dynamic_index_in_dim(owner * CAP + rank, me_obs, 0, keepdims=False)
    slot = (slot[:, None] * MP + jnp.arange(MP)[None, :]).reshape(tiles * MP, 1)
    pick = (slot == jnp.arange(obs * CAP * MP)[None, :]).astype(BF16)

    my_rows = lax.dynamic_slice_in_dim(sky.reshape(held, rows_all, LANES), me_det * mine, mine, 1)
    my_rows = jnp.pad(my_rows, ((0, 0), (0, MP - mine), (0, 0))).reshape(held * MP, LANES)
    outgoing = jnp.dot(own, my_rows, preferred_element_type=F32).reshape(obs, CAP * MP, LANES)

    wide = jnp.pad(detector_kernel.reshape(dets, det, mine), ((0, 0), (0, 0), (0, MP - mine)))
    ke = jnp.eye(4, dtype=BF16)[:, None, None, :, None] * wide[None, :, :, None, :]
    ke = ke.reshape(4 * dets, det * 16)
    sel = np.zeros((4, det, mine, det, 4, MP), np.float32)
    for q in range(4):
        for j in range(det):
            for m in range(mine):
                sel[q, j, m, j, q, m] = 1
    sel = jnp.asarray(sel.reshape(4 * rows_all, det * 16), BF16)

    block = along[0]
    n = det // 2
    scan = call(
        functools.partial(fetch_kernel, obs, det),
        jax.ShapeDtypeStruct((det, tiles * MP, LANES), BF16),
        [
            pltpu.VMEM((obs, CAP * MP, LANES), F32),
            pltpu.VMEM((tiles * MP, LANES), BF16),
            *dma(obs),
            *dma(n),
            *dma(n),
        ],
        "fetch",
        0,
    )(outgoing, pick, block)
    spectra = call(
        functools.partial(forward_kernel, det),
        jax.ShapeDtypeStruct((det, dets, 2 * FAST), BF16),
        [
            pltpu.VMEM((tiles, dets, LANES), F32),
            pltpu.VMEM((det, dets, FAST), BF16),
            pltpu.VMEM((det, dets, 2 * FAST), F32),
        ],
        "forward",
    )(ke, scan, sample_weight, fwd, tw)
    banded = call(
        functools.partial(spread_kernel, det),
        jax.ShapeDtypeStruct((det, dets, 2 * FAST), BF16),
        dma(det),
        "spread",
        1,
    )(spectra)
    mixed = call(
        functools.partial(mix_kernel, det, dets),
        jax.ShapeDtypeStruct((det, dets, 2 * FAST), BF16),
        [pltpu.VMEM((det - 1, dets, 2 * FAST), BF16), *dma(det)],
        "mix",
        2,
    )(noise, banded.reshape(all_dets, 2 * FAST))
    given = call(
        functools.partial(inverse_kernel, det),
        jax.ShapeDtypeStruct((det, tiles * MP, LANES), BF16),
        [pltpu.VMEM((det, dets, 2 * FAST), BF16), pltpu.VMEM((tiles, dets, LANES), F32)],
        "inverse",
    )(mixed, sample_weight, ke, inv, tw)
    normal = call(
        functools.partial(give_kernel, obs, det),
        jax.ShapeDtypeStruct((held, rows_all, LANES), F32),
        [
            pltpu.VMEM((det, tiles * MP, LANES), BF16),
            pltpu.VMEM((tiles * MP, LANES), F32),
            pltpu.VMEM((tiles * MP, LANES), F32),
            pltpu.VMEM((obs, CAP * MP, LANES), F32),
            pltpu.VMEM((obs, CAP * MP, LANES), F32),
            pltpu.VMEM((det, held * MP, LANES), BF16),
            *dma(det),
            *dma(obs),
            *dma(n),
            *dma(n),
        ],
        "give",
        3,
    )(given, block, pick, own, sel)
    return normal.reshape(sky.shape)


def solution(mesh):
    in_specs = (
        P("obs", None, None, None),
        P(),
        P("obs", None, None, None),
        P("det", None),
        P("det", "obs"),
        P("det", "obs", None),
    )
    out_specs = P("obs", None, None, None)
    return jax.shard_map(local, mesh=mesh, in_specs=in_specs, out_specs=out_specs, check_vma=False)
```

time: 433 us -> 212 us (0.49); the launches traced: 428 us -> 212 us
  Pallas kernels: 0 us -> 188 us
  blocking collectives: 157 us -> 0 us
  waiting for transfers between devices: 131 us -> 0.71 us
  local copies, waits for them, and re-layouts: 85.4 us -> 4.45 us
  matrix products: 27.1 us -> 0.87 us
  starting transfers between devices: 10.5 us -> 0.01 us
    pallas_call x0 -> x6, Pallas kernels: none -> 188 us  [run(): pl.pallas_call(kernel, out_shape=out, in_specs=[VMEM] * len(args), out_sp...]
    all_to_all x3 -> x0, blocking collectives: 157 us -> none  [the longest x1 68.2 us: local(): lax.all_to_all(spectra, 'det', split_axis=3, concat_axis=0, tiled=True)]
    psum x1 -> x0, waiting for transfers between devices: 110 us -> none  [local(): summed = lax.psum(tile_terms, 'det')]
    unnamed x17 -> x3, local copies, waits for them, and re-layouts: 39.8 us -> 2.07 us
    dot_general x20 -> x1, matrix products: 27.1 us -> 0.87 us  [local(): jnp.dot(own, my_rows, preferred_element_type=F32)]
    reshape x3 -> x1, local copies, waits for them, and re-layouts: 23 us -> 0.73 us  [local(): detector_kernel.reshape(dets, det, mine)]
    all_to_all x1 -> x0, waiting for transfers between devices: 20.2 us -> none  [local(): lax.all_to_all(outgoing, 'obs', split_axis=0, concat_axis=0, tiled=True)]
    all_to_all x2 -> x0, local copies, waits for them, and re-layouts: 14 us -> none  [the longest x1 12.6 us: local(): lax.all_to_all(mixed, 'det', split_axis=0, concat_axis=3, tiled=True)]
  transfers between devices with their start and end apart: 3 -> 1, of which waited for: 2 -> 0; matrix products, arithmetic and copies ran while one was open for 5% -> 4% of each run, Pallas kernels for 0% -> 41%
where the time goes in v1:
time: 212 us
  Pallas kernels  188 us (89%)
  between operations  13.5 us (6%)
  local copies, waits for them, and re-layouts  4.45 us (2%)
  other arithmetic  4.19 us (2%)
    pallas_call x6, Pallas kernels, run(): pl.pallas_call(kernel, out_shape=out, in_specs=[VMEM] * len(args), out_sp...  188 us
  transfers between devices with their start and end apart: 1, of which 0 were waited for; matrix products, arithmetic and copies ran while one was open for 4% of the time, Pallas kernels for 41%

profile of v1, /device:TPU:1, one launch (start us, length us, event | category | flops | bytes accessed | tf_op | source)
XLA Modules:
  0.0 211.8 jit_solution(16715128032692404444)
XLA Ops:
  6.5 0.0 copy-start
  6.5 0.0 all-gather.2.cloned.1.call-start
  6.5 0.7 all-gather.2.cloned.1.call-update
  7.3 0.7 broadcast_compare_fusion
  8.0 0.8 convert_reduce_fusion
  8.8 0.7 subtract_add_fusion
  9.5 0.1 select_reduce_fusion
  9.6 0.1 copy.17
  9.7 0.1 copy.16
  9.9 0.1 add_select_fusion
  10.0 0.1 copy.18
  10.1 0.1 select_n.37
  10.2 0.1 copy.19
  10.3 0.1 iota_add_fusion
  10.4 0.1 add.69
  10.5 0.7 reshape.128
  11.2 0.0 copy-done
  11.3 0.2 broadcast_multiply_fusion
  11.5 0.2 mul.53
  11.7 0.8 copy.20.ke_ref
  12.5 0.7 fusion.3.pick_ref
  13.2 0.9 fusion.1.out_ref
  14.1 33.8 %fetch.1.scan_ref = bf16[16,128,128]{2,1,0:T(8,128)(2,1)} custom-call(f32[32,8,128]{2,1,0:T(8,128)} %fusion.1.out_ref, bf16[128,256]{1,0:T(8,128)(2,1)} %fusion.3.pick_ref, bf16[32,128,128]{2,1,0:T(8,128)(2,1)} %bitcast.22), custom_call_target="tpu_custom_call" | custom-call | tf_op jit(solution)/shard_map/fetch/pallas_call | solution.py:423
  47.8 10.8 %forward.1.x_ref = bf16[16,96,512]{2,1,0:T(8,128)(2,1)} custom-call(bf16[384,256]{1,0:T(8,128)(2,1)} %copy.20.ke_ref, bf16[16,128,128]{2,1,0:T(8,128)(2,1)} %fetch.1.scan_ref, bf16[96,4096]{1,0:T(8,128)(2,1)} %w_ref.3, bf16[256,512]{1,0:T(8,128)(2,1)} %constant.57.clone.fwd_ref, f32[16,2,256]{2,1,0:T(2,128)} %constant.59.clone.tw_ref), custom_call_target="tpu_custom_call" | custom-call | tf_op jit(solution)/shard_map/forward/pallas_call | solution.py:423
  58.7 43.0 %spread.1 = bf16[16,96,512]{2,1,0:T(8,128)(2,1)} custom-call(bf16[16,96,512]{2,1,0:T(8,128)(2,1)} %forward.1.x_ref), custom_call_target="tpu_custom_call" | custom-call | tf_op jit(solution)/shard_map/spread/pallas_call | solution.py:423
  101.6 0.7 fusion.4.own_ref
  102.3 0.0 all-gather.2.cloned.1.call-done
  102.3 49.8 %mix.1.y_ref = bf16[16,96,512]{2,1,0:T(8,128)(2,1)} custom-call(bf16[1536,1536]{1,0:T(8,128)(2,1)} %bitcast.21, bf16[1536,512]{1,0:T(8,128)(2,1)} %bitcast.20), custom_call_target="tpu_custom_call" | custom-call | tf_op jit(solution)/shard_map/mix/pallas_call | solution.py:423
  152.2 11.4 %inverse.1.g_ref = bf16[16,128,128]{2,1,0:T(8,128)(2,1)} custom-call(bf16[16,96,512]{2,1,0:T(8,128)(2,1)} %mix.1.y_ref, bf16[96,4096]{1,0:T(8,128)(2,1)} %w_ref.3, bf16[384,256]{1,0:T(8,128)(2,1)} %copy.20.ke_ref, bf16[512,256]{1,0:T(8,128)(2,1)} %constant.58.clone.inv_ref, f32[16,2,256]{2,1,0:T(2,128)} %constant.59.clone.tw_ref), custom_call_target="tpu_custom_call" | custom-call | tf_op jit(solution)/shard_map/inverse/pallas_call | solution.py:423
  163.6 39.3 %give.1 = f32[32,48,128]{2,1,0:T(8,128)} custom-call(bf16[16,128,128]{2,1,0:T(8,128)(2,1)} %inverse.1.g_ref, bf16[32,128,128]{2,1,0:T(8,128)(2,1)} %bitcast.23, bf16[128,256]{1,0:T(8,128)(2,1)} %fusion.3.pick_ref, bf16[256,128]{1,0:T(8,128)(2,1)} %fusion.4.own_ref, bf16[192,256]{1,0:T(8,128)(2,1)} %constant.60.clone.sel_ref), custom_call_target="tpu_custom_call" | custom-call | tf_op jit(solution)/shard_map/give/pallas_call | solution.py:423
  202.9 2.1 copy.23
  (7 shorter events, 0.1 us)
Async XLA Ops:
  6.5 4.7 %copy-start = (bf16[32,3,16,128]{3,2,1,0:T(8,128)(2,1)S(1)}, bf16[32,3,16,128]{3,2,1,0:T(8,128)(2,1)}, u32[]{:S(2)}) copy-start(bf16[32,3,16,128]{3,2,1,0:T(8,128)(2,1)} %param.10) | copy-start | bytes 1179652
  6.5 95.8 %all-gather.2.cloned.1.call-start = ((), (), s32[]{:S(2)}) async-start(), calls=%async_computation | async-start | bytes 4866048 | tf_op jit(solution)/shard_map/all_gather | solution.py:449
Sparse Core Ops, SparseCore 0:
  10.5 90.3 all-gather.1

commit v2 on v1

--- a/solution.py
+++ b/solution.py
@@ -19,22 +19,38 @@
 VMEM = pl.BlockSpec(memory_space=pltpu.VMEM)
 
 
+def band_of(slot, det):
+    return slot if slot % 2 == 0 else det - slot
+
+
 def tables(slow):
     lane = np.arange(FAST)
     half, rest = lane // LANES, lane % LANES
     j, i = rest // slow, rest % slow
     w = half * LANES + i * (LANES // slow) + j
-    r = np.arange(FAST)
+    r = np.arange(LANES)
     angle = 2 * np.pi / FAST * (w[:, None] * r[None, :] % FAST)
     c, s = np.cos(angle) / math.sqrt(FAST), np.sin(angle) / math.sqrt(FAST)
     forward = np.concatenate([c, -s], 1)
-    inverse = np.concatenate([c.T, -s.T], 0)
+    keep = (r > 0)[:, None]
+    inverse = np.concatenate([c.T * keep, -s.T * keep], 0)
     twist = 2 * np.pi / (slow * FAST) * (np.arange(slow)[:, None] * r[None, :])
     tw = np.stack([np.cos(twist), np.sin(twist)], 1) / math.sqrt(slow)
+    edge = np.zeros((slow, 8, slow, 8))
+    for slot in range(slow):
+        for v in range(2):
+            turn = 2 * np.pi / slow * (band_of(slot, slow) + v / 2) * np.arange(slow)
+            edge[slot, 2 * v, :, v] = np.cos(turn) / math.sqrt(slow)
+            edge[slot, 2 * v + 1, :, v] = -np.sin(turn) / math.sqrt(slow)
+    ends = np.zeros((8, FAST))
+    ends[0] = 1 / math.sqrt(FAST)
+    ends[1] = (1 - 2 * (w % 2)) / math.sqrt(FAST)
     return (
         jnp.asarray(forward, BF16),
         jnp.asarray(inverse, BF16),
-        jnp.asarray(tw.reshape(slow, 2, FAST), F32),
+        jnp.asarray(tw, F32),
+        jnp.asarray(edge.reshape(8 * slow, 8 * slow), BF16),
+        jnp.asarray(ends, BF16),
     )
 
 
@@ -206,9 +222,17 @@
     det_gather(det, scan_ref, sems)
 
 
-def forward_kernel(slow, ke_ref, scan_ref, w_ref, fwd_ref, tw_ref, x_ref, ts, u, half):
+def place(slot_band, b):
+    slot = slot_band.index(b)
+    return slot // 2, (slot % 2) * FAST
+
+
+def forward_kernel(
+    slow, ke_ref, scan_ref, w_ref, fwd_ref, tw_ref, edge_ref, ends_ref, x_ref, e_ref, ts, u, half, sums
+):
     dets = w_ref.shape[0]
     tiles = w_ref.shape[1] // LANES
+    bands = [band_of(slot, slow) for slot in range(slow)]
     for i in range(tiles // 4):
         rhs = scan_ref[:, 16 * i : 16 * i + 16, :].reshape(slow * 16, LANES)
         rows = jnp.dot(ke_ref[...], rhs, preferred_element_type=F32)
@@ -227,53 +251,73 @@
 
         lax.fori_loop(0, dets // 16, swap, 0)
 
+    sums[...] = jnp.zeros_like(sums)
+
     def fast(z, carry):
         a = jnp.dot(u[z], fwd_ref[...], preferred_element_type=F32)
-        re, im = a[:, :FAST], a[:, FAST:]
+        re, im = a[:, :LANES], a[:, LANES:]
         c, s = tw_ref[z, 0:1, :], tw_ref[z, 1:2, :]
-        half[z, :, :FAST] = re * c + im * s
-        half[z, :, FAST:] = im * c - re * s
+        half[z, :, :LANES] = re * c + im * s
+        half[z, :, LANES:] = im * c - re * s
+        sums[pl.ds(pl.multiple_of(z * 8, 8), 8), :dets] = lax.dot_general(
+            ends_ref[...], u[z], (((1,), (1,)), ((), ())), preferred_element_type=F32
+        )
         return carry
 
     lax.fori_loop(0, slow, fast, 0)
-
-    for rc in range(2):
-        lo, hi = rc * LANES, FAST + rc * LANES
-
-        def last(g, carry):
-            at = pl.ds(pl.multiple_of(g * 16, 16), 16)
-            re = [half[z, at, lo : lo + LANES] for z in range(slow)]
-            im = [half[z, at, hi : hi + LANES] for z in range(slow)]
-            re, im = small_dft(re, im, -1)
-            for b in range(slow):
-                x_ref[b, at, lo : lo + LANES] = re[b].astype(BF16)
-                x_ref[b, at, hi : hi + LANES] = im[b].astype(BF16)
-            return carry
-
-        lax.fori_loop(0, dets // 16, last, 0)
-
-
-def inverse_kernel(slow, y_ref, w_ref, ke_ref, inv_ref, tw_ref, g_ref, turned, ts):
+    e_ref[...] = split_dot(edge_ref[...], sums[...], ROWS_COLS)
+
+    def last(g, carry):
+        at = pl.ds(pl.multiple_of(g * 16, 16), 16)
+        re = [half[z, at, :LANES] for z in range(slow)]
+        im = [half[z, at, LANES:] for z in range(slow)]
+        re, im = small_dft(re, im, -1)
+        for b in range(slow):
+            chip, lo = place(bands, b)
+            x_ref[chip, at, lo : lo + LANES] = re[b].astype(BF16)
+            x_ref[chip, at, lo + LANES : lo + FAST] = im[b].astype(BF16)
+        return carry
+
+    lax.fori_loop(0, dets // 16, last, 0)
+
+
+def inverse_kernel(
+    slow, y_ref, e_ref, w_ref, ke_ref, inv_ref, tw_ref, edge_ref, ends_ref, g_ref, turned, ts, sums
+):
     dets = w_ref.shape[0]
     tiles = w_ref.shape[1] // LANES
-    for rc in range(2):
-        lo, hi = rc * LANES, FAST + rc * LANES
-
-        def first(g, carry):
-            at = pl.ds(pl.multiple_of(g * 16, 16), 16)
-            re = [y_ref[b, at, lo : lo + LANES].astype(F32) for b in range(slow)]
-            im = [y_ref[b, at, hi : hi + LANES].astype(F32) for b in range(slow)]
-            re, im = small_dft(re, im, 1)
-            for z in range(slow):
-                c, s = tw_ref[z, 0:1, lo : lo + LANES], tw_ref[z, 1:2, lo : lo + LANES]
-                turned[z, at, lo : lo + LANES] = (re[z] * c - im[z] * s).astype(BF16)
-                turned[z, at, hi : hi + LANES] = (im[z] * c + re[z] * s).astype(BF16)
-            return carry
-
-        lax.fori_loop(0, dets // 16, first, 0)
+    bands = [band_of(slot, slow) for slot in range(slow)]
+
+    def first(g, carry):
+        at = pl.ds(pl.multiple_of(g * 16, 16), 16)
+        re, im = [], []
+        for b in range(slow):
+            chip, lo = place(bands, b)
+            re.append(y_ref[chip, at, lo : lo + LANES].astype(F32))
+            im.append(y_ref[chip, at, lo + LANES : lo + FAST].astype(F32))
+        re, im = small_dft(re, im, 1)
+        for z in range(slow):
+            c, s = tw_ref[z, 0:1, :], tw_ref[z, 1:2, :]
+            turned[z, at, :LANES] = (re[z] * c - im[z] * s).astype(BF16)
+            turned[z, at, LANES:] = (im[z] * c + re[z] * s).astype(BF16)
+        return carry
+
+    lax.fori_loop(0, dets // 16, first, 0)
+    part = dets // 2
+    for q in range(2):
+        rows = e_ref[:, q].reshape(8 * slow, LANES)
+        sums[q] = split_dot(edge_ref[...], rows, COLS_COLS).astype(BF16).astype(F32)
 
     def fast(z, carry):
         o = jnp.dot(turned[z], inv_ref[...], preferred_element_type=F32)
+        at = pl.ds(pl.multiple_of(z * 8, 8), 8)
+        edge = [
+            lax.dot_general(
+                sums[q, at, :].astype(BF16), ends_ref[...], COLS_COLS, preferred_element_type=F32
+            )[:part]
+            for q in range(2)
+        ]
+        o = o + jnp.concatenate(edge, 0)
         ts[z] = o[:, :LANES]
         ts[slow + z] = o[:, LANES:]
         return carry
@@ -307,59 +351,189 @@
     return [lax.rem(me + d, det) for d in range(1, det)]
 
 
-def spread_kernel(det, x_ref, out_ref, send_sem, recv_sem):
+def det_send(src, dst, send_sem, recv_sem, to):
+    return pltpu.make_async_remote_copy(
+        src_ref=src,
+        dst_ref=dst,
+        send_sem=send_sem,
+        recv_sem=recv_sem,
+        device_id={"det": to},
+        device_id_type=MESH,
+    )
+
+
+def far_first(n):
+    return sorted(range(n), key=lambda d: -min(d, n - d))
+
+
+def spread_kernel(
+    obs, det, x_ref, e_ref, np_ref, out_ref, eout_ref,
+    es, payload, gathered, wide, zs, zr, xs0, xs1, es0, es1, gs0, gs1, zs0, zs1, fs0, fs1,
+):
     me = lax.axis_index("det")
+    block = lax.axis_index("obs")
+    n = det // 2
+    chip = me // 2
+    side = me // n
     peers = all_det(det)
-    greet(0, det, False, peers)
-    copies = []
-    for d in sorted(range(1, det), key=lambda d: -min(d, det - d)):
-        copies.append(
-            pltpu.make_async_remote_copy(
-                src_ref=x_ref.at[peers[d - 1]],
-                dst_ref=out_ref.at[me],
-                send_sem=send_sem.at[d],
-                recv_sem=recv_sem.at[d],
-                device_id={"det": peers[d - 1]},
-                device_id_type=MESH,
+    greet(obs, det, True, peers)
+
+    edges = []
+    for d in range(1, det):
+        to = peers[d - 1]
+        edges.append(
+            det_send(
+                e_ref.at[pl.ds(pl.multiple_of(to * 8, 8), 8)],
+                es.at[pl.ds(pl.multiple_of(me * 8, 8), 8)],
+                es0.at[d],
+                es1.at[d],
+                to,
             )
         )
-        copies[-1].start()
-    out_ref[me] = x_ref[me]
-    for copy in copies:
+        edges[-1].start()
+
+    slot = lax.rem(me, n)
+
+    def column(d):
+        to_chip = lax.rem(chip + d, n)
+        return det_send(x_ref.at[to_chip], out_ref.at[slot], xs0.at[d], xs1.at[slot], to_chip * 2 + side)
+
+    for d in far_first(n)[:-1]:
+        column(d).start()
+    mine = lax.rem(me, 2) == side
+
+    @pl.when(mine)
+    def _():
+        out_ref[slot] = x_ref[chip]
+
+    @pl.when(jnp.logical_not(mine))
+    def _():
+        column(0).start()
+
+    own = pl.ds(pl.multiple_of(me * 8, 8), 8)
+    es[own, :] = e_ref[own, :]
+    for copy in edges:
         copy.wait()
-
-
-def mix_kernel(det, dets, n_ref, x_ref, out_ref, staged, send_sem, recv_sem):
+    for i in range(4):
+        payload[16 * i : 16 * i + det] = es[pl.ds(i, det, stride=8), :].astype(BF16)
+
+    def give(d):
+        to = lax.rem(block + d, obs)
+        return pltpu.make_async_remote_copy(
+            src_ref=payload,
+            dst_ref=gathered.at[block],
+            send_sem=gs0.at[d],
+            recv_sem=gs1.at[d],
+            device_id={"obs": to},
+            device_id_type=MESH,
+        )
+
+    def start(d, carry):
+        give(d).start()
+        return carry
+
+    def wait(d, carry):
+        give(d).wait()
+        return carry
+
+    lax.fori_loop(1, obs, start, 0)
+    gathered[block] = payload[...]
+    lax.fori_loop(1, obs, wait, 0)
+    wide[...] = gathered[...].reshape(obs * 64, LANES).astype(F32)
+    got = jnp.zeros((obs * 4, np_ref.shape[1]), F32)
+    for j in range(det):
+        rows = wide[pl.ds(j, obs * 4, stride=16), :].astype(BF16)
+        got = got + lax.dot_general(rows, np_ref[j], (((1,), (1,)), ((), ())), preferred_element_type=F32)
+    zs[...] = jnp.zeros_like(zs)
+    for p in range(obs):
+        zs[p, 0:4, : np_ref.shape[1]] = got[4 * p : 4 * p + 4]
+    obs_exchange(obs, zs, zr, zs0, zs1)
+    per = obs // det
+    finals = []
+    for d in range(1, det):
+        to = peers[d - 1]
+        finals.append(
+            det_send(zr.at[pl.ds(to * per, per)], eout_ref.at[me], fs0.at[d], fs1.at[d], to)
+        )
+        finals[-1].start()
+    eout_ref[me] = zr[pl.ds(me * per, per)]
+
+    for d in far_first(n)[:-1]:
+        column(d).wait_send()
+
+    @pl.when(jnp.logical_not(mine))
+    def _():
+        column(0).wait_send()
+
+    home = lax.rem(me, 2) * n
+    for i in range(n):
+
+        @pl.when(home + i != me)
+        def _():
+            det_send(out_ref.at[i], out_ref.at[i], xs0.at[0], xs1.at[i], me).wait_recv()
+
+    for copy in finals:
+        copy.wait()
+
+
+def mix_kernel(det, dets, m_ref, x_ref, out_ref, given, taken, staged, ps0, ps1, ys0, ys1):
     me = lax.axis_index("det")
-    peers = all_det(det) + [me]
-    greet(0, det, False, peers[:-1])
-    copies = []
-    for s in range(0, det, 4):
-        rows = [
-            n_ref[pl.ds(pl.multiple_of(to * dets, 16), dets), :] for to in peers[s : s + 4]
-        ]
-        got = jnp.dot(jnp.concatenate(rows, 0), x_ref[...], preferred_element_type=F32)
-        got = got.astype(BF16)
-        for i in range(4):
-            d = s + i + 1
-            block = got[i * dets : (i + 1) * dets]
-            if d == det:
-                out_ref[me] = block
-                continue
-            staged[d - 1] = block
-            copies.append(
-                pltpu.make_async_remote_copy(
-                    src_ref=staged.at[d - 1],
-                    dst_ref=out_ref.at[me],
-                    send_sem=send_sem.at[d],
-                    recv_sem=recv_sem.at[d],
-                    device_id={"det": peers[d - 1]},
-                    device_id_type=MESH,
-                )
-            )
-            copies[-1].start()
-    for copy in copies:
-        copy.wait()
+    n = det // 2
+    chip = me // 2
+    core = lax.rem(me, 2)
+    partner = me + 1 - 2 * core
+    half = n // 2
+    greet(0, det, False, all_det(det))
+    swaps, sends = [], []
+
+    def product(to_chip):
+        rows = m_ref[pl.ds(pl.multiple_of(to_chip * 2 * dets, 16), 2 * dets), :]
+        return jnp.dot(rows, x_ref[...], preferred_element_type=F32)
+
+    def finish(s, total):
+        to_chip = core * half + lax.rem(chip + s, half)
+        swaps[s].wait_recv()
+        total = total + taken[s].astype(F32)
+        for i in range(2):
+            to = to_chip * 2 + i
+            staged[s, i] = total[i * dets : (i + 1) * dets].astype(BF16)
+            copy = det_send(staged.at[s, i], out_ref.at[chip], ys0.at[s, i], ys1.at[chip], to)
+
+            @pl.when(to != me)
+            def _():
+                copy.start()
+
+            @pl.when(to == me)
+            def _():
+                out_ref[chip] = staged[s, i]
+
+            sends.append((to, copy))
+
+    before = None
+    for s in range(half):
+        near = lax.rem(chip + s, half)
+        given[s] = product((1 - core) * half + near).astype(BF16)
+        swaps.append(det_send(given.at[s], taken.at[s], ps0.at[s], ps1.at[s], partner))
+        swaps[-1].start()
+        total = product(core * half + near)
+        if before is not None:
+            finish(s - 1, before)
+        before = total
+    finish(half - 1, before)
+    side = me // n
+    for c in range(n):
+
+        @pl.when(c * 2 + side != me)
+        def _():
+            det_send(out_ref.at[c], out_ref.at[c], ys0.at[0, 0], ys1.at[c], me).wait_recv()
+
+    for copy in swaps:
+        copy.wait_send()
+    for to, copy in sends:
+
+        @pl.when(to != me)
+        def _():
+            copy.wait_send()
 
 
 def give_kernel(
@@ -424,7 +598,7 @@
             kernel,
             out_shape=out,
             in_specs=[VMEM] * len(args),
-            out_specs=VMEM,
+            out_specs=VMEM if not isinstance(out, tuple) else (VMEM,) * len(out),
             scratch_shapes=scratch,
             compiler_params=params,
             name=name,
@@ -444,9 +618,22 @@
     dets, all_dets = detector_kernel.shape[0], noise_inverse.shape[2]
     rows_all = sky.shape[1] * sky.shape[2]
     mine = rows_all // det
-    fwd, inv, tw = tables(det)
-
-    noise = lax.all_gather(noise_inverse, "obs", axis=1, tiled=True)[0]
+    fwd, inv, tw, edge, ends = tables(det)
+
+    rows = noise_inverse[0]
+    part = all_dets // 2
+    core = me_det % 2
+    odd = core == 1
+    swapped = lax.ppermute(rows, "det", [(j, det - j) for j in range(1, det, 2)])
+    offered = jnp.where(odd, rows[:, :part], rows[:, part:])
+    ways = [(j, det - 1 - j if j % 2 else j + 1) for j in range(det)]
+    other = lax.ppermute(offered, "det", ways)
+    rows = jnp.where(odd, swapped, rows)
+    both = jnp.where(odd, rows[:, part:], rows[:, :part]).astype(F32) + other.astype(F32)
+    folded = lax.all_gather(both.astype(BF16), "obs", axis=0, tiled=True)
+    spread_rows = jnp.pad(
+        rows.reshape(-1, det, dets), ((0, 0), (0, 0), (0, LANES - dets))
+    ).transpose(1, 0, 2)
 
     owner = tile_list // held
     earlier = jnp.arange(tiles)[None, :] < jnp.arange(tiles)[:, None]
@@ -495,36 +682,68 @@
         "fetch",
         0,
     )(outgoing, pick, block)
-    spectra = call(
+    spectra, edges = call(
         functools.partial(forward_kernel, det),
-        jax.ShapeDtypeStruct((det, dets, 2 * FAST), BF16),
+        (
+            jax.ShapeDtypeStruct((n, dets, 2 * FAST), BF16),
+            jax.ShapeDtypeStruct((8 * det, LANES), F32),
+        ),
         [
             pltpu.VMEM((tiles, dets, LANES), F32),
             pltpu.VMEM((det, dets, FAST), BF16),
-            pltpu.VMEM((det, dets, 2 * FAST), F32),
+            pltpu.VMEM((det, dets, FAST), F32),
+            pltpu.VMEM((8 * det, LANES), F32),
         ],
         "forward",
-    )(ke, scan, sample_weight, fwd, tw)
-    banded = call(
-        functools.partial(spread_kernel, det),
-        jax.ShapeDtypeStruct((det, dets, 2 * FAST), BF16),
-        dma(det),
+    )(ke, scan, sample_weight, fwd, tw, edge, ends)
+    per = obs // det
+    banded, edges = call(
+        functools.partial(spread_kernel, obs, det),
+        (
+            jax.ShapeDtypeStruct((n, dets, 2 * FAST), BF16),
+            jax.ShapeDtypeStruct((det, per, 8, LANES), F32),
+        ),
+        [
+            pltpu.VMEM((8 * det, LANES), F32),
+            pltpu.VMEM((64, LANES), BF16),
+            pltpu.VMEM((obs, 64, LANES), BF16),
+            pltpu.VMEM((obs * 64, LANES), F32),
+            pltpu.VMEM((obs, 8, LANES), F32),
+            pltpu.VMEM((obs, 8, LANES), F32),
+            *dma(n),
+            *dma(det),
+            *dma(obs),
+            *dma(obs),
+            *dma(det),
+        ],
         "spread",
         1,
-    )(spectra)
+    )(spectra, edges, spread_rows)
+    half = n // 2
     mixed = call(
         functools.partial(mix_kernel, det, dets),
-        jax.ShapeDtypeStruct((det, dets, 2 * FAST), BF16),
-        [pltpu.VMEM((det - 1, dets, 2 * FAST), BF16), *dma(det)],
+        jax.ShapeDtypeStruct((n, dets, 2 * FAST), BF16),
+        [
+            pltpu.VMEM((half, 2 * dets, 2 * FAST), BF16),
+            pltpu.VMEM((half, 2 * dets, 2 * FAST), BF16),
+            pltpu.VMEM((half, 2, dets, 2 * FAST), BF16),
+            *dma(half),
+            pltpu.SemaphoreType.DMA((half, 2)),
+            pltpu.SemaphoreType.DMA((n,)),
+        ],
         "mix",
         2,
-    )(noise, banded.reshape(all_dets, 2 * FAST))
+    )(folded, banded.reshape(n * dets, 2 * FAST))
     given = call(
         functools.partial(inverse_kernel, det),
         jax.ShapeDtypeStruct((det, tiles * MP, LANES), BF16),
-        [pltpu.VMEM((det, dets, 2 * FAST), BF16), pltpu.VMEM((tiles, dets, LANES), F32)],
+        [
+            pltpu.VMEM((det, dets, FAST), BF16),
+            pltpu.VMEM((tiles, dets, LANES), F32),
+            pltpu.VMEM((2, 8 * det, LANES), F32),
+        ],
         "inverse",
-    )(mixed, sample_weight, ke, inv, tw)
+    )(mixed, edges, sample_weight, ke, inv, tw, edge, ends)
     normal = call(
         functools.partial(give_kernel, obs, det),
         jax.ShapeDtypeStruct((held, rows_all, LANES), F32),

time: 212 us -> 213 us (level)
  Pallas kernels: 188 us -> 170 us
  starting transfers between devices: 0.01 us -> 13.5 us
  other arithmetic: 4.19 us -> 6.7 us
    pallas_call x6, Pallas kernels: 188 us -> 170 us  [run(): pl.pallas_call(kernel, out_shape=out, in_specs=[VMEM] * len(args), out_sp...]
    ppermute x0 -> x2, starting transfers between devices: none -> 13.5 us  [the longest x1 11.6 us: local(): lax.ppermute(rows, 'det', [(j, det - j) for j in range(1, det, 2)])]
    ppermute x0 -> x2, waiting for transfers between devices: none -> 2.21 us  [the longest x1 2.21 us: local(): lax.ppermute(rows, 'det', [(j, det - j) for j in range(1, det, 2)])]
  transfers between devices with their start and end apart: 1 -> 3, of which waited for: 0 -> 1; matrix products, arithmetic and copies ran while one was open for 4% -> 5% of each run, Pallas kernels for 41% -> 43%
where the time goes in v2:
time: 213 us; the launch traced here: 212 us
  Pallas kernels  170 us (80%)
  between operations  13.6 us (6%)
  starting transfers between devices  13.5 us (6%)
  other arithmetic  6.7 us (3%)
  local copies, waits for them, and re-layouts  5.41 us (3%)
  waiting for transfers between devices  2.25 us (1%)
    pallas_call x6, Pallas kernels, run(): pl.pallas_call(kernel, out_shape=out, in_specs=[VMEM] * len(args), out_sp...  170 us
    ppermute x1, starting transfers between devices, local(): lax.ppermute(rows, 'det', [(j, det - j) for j in range(1, det, 2)])  11.6 us
  transfers between devices with their start and end apart: 3, of which 1 were waited for; matrix products, arithmetic and copies ran while one was open for 5% of the time, Pallas kernels for 43%

profile of v2, /device:TPU:1, one launch (start us, length us, event | category | flops | bytes accessed | tf_op | source)
XLA Modules:
  0.0 211.9 jit_solution(7470182675113716896)
XLA Ops:
  6.5 0.0 copy-start
  6.5 0.0 all-gather.2.cloned.1.call-start
  6.5 11.6 %collective-permute-start = (bf16[48,1536]{1,0:T(8,128)(2,1)}, bf16[48,1536]{1,0:T(8,128)(2,1)S(1)}, u32[]{:S(2)}, u32[]{:S(2)}) collective-permute-start(bf16[48,1536]{1,0:T(8,128)(2,1)} %bitcast.27), channel_id=1, source_target_pairs={{1,15},{3,13},{5,11},{7,9},{9,7},{11,5},{13,3},{15,1},{17,31},{19,... | collective-permute-start | bytes 442376 | tf_op jit(solution)/shard_map/ppermute | solution.py:627
  18.2 0.9 slice_select_fusion
  19.1 1.9 collective-permute-start.1
  21.0 2.2 %collective-permute-done = bf16[48,1536]{1,0:T(8,128)(2,1)S(1)} collective-permute-done((bf16[48,1536]{1,0:T(8,128)(2,1)}, bf16[48,1536]{1,0:T(8,128)(2,1)S(1)}, u32[]{:S(2)}, u32[]{:S(2)}) %collective-permute-start) | collective-permute-done | bytes 147488 | tf_op jit(solution)/shard_map/ppermute | solution.py:627
  23.2 0.9 broadcast_select_fusion
  24.2 0.0 collective-permute-done.1
  24.2 0.7 add_convert_fusion
  24.8 0.0 all-gather.2.cloned.1.call-update
  24.9 0.7 broadcast_compare_fusion
  25.6 0.8 convert_reduce_fusion
  26.4 0.7 subtract_add_fusion
  27.1 0.1 select_reduce_fusion
  27.3 0.1 copy.21
  27.4 0.1 copy.20
  27.5 0.1 add_select_fusion
  27.6 0.1 copy.22
  27.7 0.1 select_n.70
  27.8 0.1 copy.23
  27.9 0.1 iota_add_fusion
  28.0 0.1 add.80
  28.1 0.7 reshape.131
  28.8 0.0 copy-done
  28.9 0.2 broadcast_multiply_fusion
  29.1 0.2 mul.53
  29.3 0.8 copy.24.ke_ref
  30.1 0.7 fusion.3.pick_ref
  30.8 0.9 fusion.1.out_ref
  31.7 26.4 %fetch.1.scan_ref = bf16[16,128,128]{2,1,0:T(8,128)(2,1)} custom-call(f32[32,8,128]{2,1,0:T(8,128)} %fusion.1.out_ref, bf16[128,256]{1,0:T(8,128)(2,1)} %fusion.3.pick_ref, bf16[32,128,128]{2,1,0:T(8,128)(2,1)} %bitcast.23), custom_call_target="tpu_custom_call" | custom-call | tf_op jit(solution)/shard_map/fetch/pallas_call | solution.py:597
  58.1 10.0 %forward.1 = (bf16[8,96,512]{2,1,0:T(8,128)(2,1)}, f32[128,128]{1,0:T(8,128)}) custom-call(bf16[384,256]{1,0:T(8,128)(2,1)} %copy.24.ke_ref, bf16[16,128,128]{2,1,0:T(8,128)(2,1)} %fetch.1.scan_ref, bf16[96,4096]{1,0:T(8,128)(2,1)} %w_ref.3, bf16[256,256]{1,0:T(8,128)(2,1)} %constant.72.clone.fwd_ref, f32[16,2,128]{2,1,0:T(2,128)} %constant.74.clone.tw_ref, ...), custom_call_target="tpu_custom_call" | custom-call | tf_op jit(solution)/shard_map/forward/pallas_call | solution.py:597
  68.1 0.7 fusion.4.own_ref
  68.8 0.2 reshape.134
  69.0 0.1 copy.25
  69.1 0.7 pad_bitcast_fusion.np_ref
  69.8 54.5 %spread.1 = (bf16[8,96,512]{2,1,0:T(8,128)(2,1)}, f32[16,2,8,128]{3,2,1,0:T(8,128)}) custom-call(bf16[8,96,512]{2,1,0:T(8,128)(2,1)} %get-tuple-element.9.x_ref, f32[128,128]{1,0:T(8,128)} %get-tuple-element.10.e_ref, bf16[16,48,128]{2,1,0:T(8,128)(2,1)} %pad_bitcast_fusion.np_ref), custom_call_target="tpu_custom_call" | custom-call | tf_op jit(solution)/shard_map/spread/pallas_call | solution.py:597
  124.3 0.0 all-gather.2.cloned.1.call-done.m_ref
  124.3 24.9 %mix.1.y_ref = bf16[8,96,512]{2,1,0:T(8,128)(2,1)} custom-call(bf16[1536,768]{1,0:T(8,128)(2,1)} %all-gather.2.cloned.1.call-done.m_ref, bf16[768,512]{1,0:T(8,128)(2,1)} %bitcast.26), custom_call_target="tpu_custom_call" | custom-call | tf_op jit(solution)/shard_map/mix/pallas_call | solution.py:597
  149.2 11.8 %inverse.1.g_ref = bf16[16,128,128]{2,1,0:T(8,128)(2,1)} custom-call(bf16[8,96,512]{2,1,0:T(8,128)(2,1)} %mix.1.y_ref, f32[16,2,8,128]{3,2,1,0:T(8,128)} %get-tuple-element.12.e_ref, bf16[96,4096]{1,0:T(8,128)(2,1)} %w_ref.3, bf16[384,256]{1,0:T(8,128)(2,1)} %copy.24.ke_ref, bf16[256,256]{1,0:T(8,128)(2,1)} %constant.73.clone.inv_ref, ...), custom_call_target="tpu_custom_call" | custom-call | tf_op jit(solution)/shard_map/inverse/pallas_call | solution.py:597
  161.0 42.0 %give.1 = f32[32,48,128]{2,1,0:T(8,128)} custom-call(bf16[16,128,128]{2,1,0:T(8,128)(2,1)} %inverse.1.g_ref, bf16[32,128,128]{2,1,0:T(8,128)(2,1)} %bitcast.24, bf16[128,256]{1,0:T(8,128)(2,1)} %fusion.3.pick_ref, bf16[256,128]{1,0:T(8,128)(2,1)} %fusion.4.own_ref, bf16[192,256]{1,0:T(8,128)(2,1)} %constant.77.clone.sel_ref), custom_call_target="tpu_custom_call" | custom-call | tf_op jit(solution)/shard_map/give/pallas_call | solution.py:597
  203.0 2.1 copy.28
  (7 shorter events, 0.1 us)
Async XLA Ops:
  6.5 22.3 %copy-start = (bf16[32,3,16,128]{3,2,1,0:T(8,128)(2,1)S(1)}, bf16[32,3,16,128]{3,2,1,0:T(8,128)(2,1)}, u32[]{:S(2)}) copy-start(bf16[32,3,16,128]{3,2,1,0:T(8,128)(2,1)} %param.12) | copy-start | bytes 1179652
  6.5 117.7 %all-gather.2.cloned.1.call-start = ((), (), s32[]{:S(2)}) async-start(), calls=%async_computation | async-start | bytes 2433024 | tf_op jit(solution)/shard_map/all_gather | solution.py:633
  6.5 16.7 %collective-permute-start = (bf16[48,1536]{1,0:T(8,128)(2,1)}, bf16[48,1536]{1,0:T(8,128)(2,1)S(1)}, u32[]{:S(2)}, u32[]{:S(2)}) collective-permute-start(bf16[48,1536]{1,0:T(8,128)(2,1)} %bitcast.27), channel_id=1, source_target_pairs={{1,15},{3,13},{5,11},{7,9},{9,7},{11,5},{13,3},{15,1},{17,31},{19,... | collective-permute-start | bytes 442376 | tf_op jit(solution)/shard_map/ppermute | solution.py:627
  19.1 5.1 %collective-permute-start.1 = (bf16[48,768]{1,0:T(8,128)(2,1)S(1)}, bf16[48,768]{1,0:T(8,128)(2,1)S(1)}, u32[]{:S(2)}, u32[]{:S(2)}) collective-permute-start(bf16[48,768]{1,0:T(8,128)(2,1)S(1)} %slice_select_fusion), channel_id=1, source_target_pairs={{0,1},{1,14},{2,3},{3,12},{4,5},{5,10},{6,7},{7,8},{8,9},{9,6},{10... | collective-permute-start | bytes 221192 | tf_op jit(solution)/shard_map/ppermute | solution.py:630
Sparse Core Ops, SparseCore 0:
  25.0 86.0 all-gather.1

commit v3 on v1

v3 whole, which is shorter than its diff:
```python
import functools
import math

import jax
import jax.numpy as jnp
import numpy as np
from jax import lax
from jax.experimental import pallas as pl
from jax.experimental.pallas import tpu as pltpu
from jax.sharding import PartitionSpec as P

CAP = 2
MP = 4
FAST = 256
LANES = 128
MESH = pl.DeviceIdType.MESH
F32 = jnp.float32
BF16 = jnp.bfloat16
VMEM = pl.BlockSpec(memory_space=pltpu.VMEM)


def band_of(slot, det):
    return slot if slot % 2 == 0 else det - slot


def tables(slow):
    lane = np.arange(FAST)
    half, rest = lane // LANES, lane % LANES
    j, i = rest // slow, rest % slow
    w = half * LANES + i * (LANES // slow) + j
    r = np.arange(LANES)
    angle = 2 * np.pi / FAST * (w[:, None] * r[None, :] % FAST)
    c, s = np.cos(angle) / math.sqrt(FAST), np.sin(angle) / math.sqrt(FAST)
    forward = np.concatenate([c, -s], 1)
    keep = (r > 0)[:, None]
    inverse = np.concatenate([c.T * keep, -s.T * keep], 0)
    twist = 2 * np.pi / (slow * FAST) * (np.arange(slow)[:, None] * r[None, :])
    tw = np.stack([np.cos(twist), np.sin(twist)], 1) / math.sqrt(slow)
    edge = np.zeros((slow, 8, slow, 8))
    for slot in range(slow):
        for v in range(2):
            turn = 2 * np.pi / slow * (band_of(slot, slow) + v / 2) * np.arange(slow)
            edge[slot, 2 * v, :, v] = np.cos(turn) / math.sqrt(slow)
            edge[slot, 2 * v + 1, :, v] = -np.sin(turn) / math.sqrt(slow)
    ends = np.zeros((8, FAST))
    ends[0] = 1 / math.sqrt(FAST)
    ends[1] = (1 - 2 * (w % 2)) / math.sqrt(FAST)
    return (
        jnp.asarray(forward, BF16),
        jnp.asarray(inverse, BF16),
        jnp.asarray(tw, F32),
        jnp.asarray(edge.reshape(8 * slow, 8 * slow), BF16),
        jnp.asarray(ends, BF16),
    )


def small_dft(re, im, sign):
    n = len(re)
    if n == 1:
        return re, im
    er, ei = small_dft(re[0::2], im[0::2], sign)
    odr, odi = small_dft(re[1::2], im[1::2], sign)
    outr, outi = [None] * n, [None] * n
    for k in range(n // 2):
        if k == 0:
            tr, ti = odr[0], odi[0]
        elif 4 * k == n:
            tr, ti = (-odi[k], odr[k]) if sign > 0 else (odi[k], -odr[k])
        else:
            c = math.cos(2 * math.pi * k / n)
            s = sign * math.sin(2 * math.pi * k / n)
            if 8 * k == n:
                tr, ti = (
                    c * (odr[k] - sign * odi[k]),
                    c * (odi[k] + sign * odr[k]),
                )
            else:
                tr, ti = c * odr[k] - s * odi[k], c * odi[k] + s * odr[k]
        outr[k], outi[k] = er[k] + tr, ei[k] + ti
        outr[k + n // 2], outi[k + n // 2] = er[k] - tr, ei[k] - ti
    return outr, outi


def digit_swap(tiles):
    n = len(tiles)
    tiles = list(tiles)
    lane = lax.broadcasted_iota(jnp.int32, tiles[0].shape, 1)
    step = 1
    while step < n:
        odd = (lane // step) % 2 == 1
        for i in range(n):
            if i & step:
                continue
            a, b = tiles[i], tiles[i | step]
            tiles[i] = jnp.where(odd, pltpu.roll(b, step, 1), a)
            tiles[i | step] = jnp.where(odd, b, pltpu.roll(a, LANES - step, 1))
        step *= 2
    return tiles


def greet(obs, det, with_obs, det_peers):
    barrier = pltpu.get_barrier_semaphore()
    count = 0
    if with_obs:
        me = lax.axis_index("obs")

        def signal(d, carry):
            pl.semaphore_signal(
                barrier, inc=1, device_id={"obs": lax.rem(me + d, obs)}, device_id_type=MESH
            )
            return carry

        lax.fori_loop(1, obs, signal, 0)
        count += obs - 1
    for peer in det_peers:
        pl.semaphore_signal(barrier, inc=1, device_id={"det": peer}, device_id_type=MESH)
    count += len(det_peers)
    pl.semaphore_wait(barrier, count)


def same_core(det):
    me = lax.axis_index("det")
    others = [lax.rem(me + 2 * d, det) for d in range(1, det // 2)]
    partner = me + 1 - 2 * lax.rem(me, 2)
    return others, partner


def obs_copies(obs, src, dst, send_sem, recv_sem, same=False):
    me = lax.axis_index("obs")

    def copy(d):
        to = lax.rem(me + d, obs)
        return pltpu.make_async_remote_copy(
            src_ref=src if same else src.at[to],
            dst_ref=dst.at[me],
            send_sem=send_sem.at[d],
            recv_sem=recv_sem.at[d],
            device_id={"obs": to},
            device_id_type=MESH,
        )

    def start():
        def step(d, carry):
            copy(d).start()
            return carry

        lax.fori_loop(1, obs, step, 0)
        dst[me] = src[...] if same else src[me]

    def wait():
        def step(d, carry):
            copy(d).wait()
            return carry

        lax.fori_loop(1, obs, step, 0)

    return start, wait


def det_send(src, dst, send_sem, recv_sem, to):
    return pltpu.make_async_remote_copy(
        src_ref=src,
        dst_ref=dst,
        send_sem=send_sem,
        recv_sem=recv_sem,
        device_id={"det": to},
        device_id_type=MESH,
    )


def far_first(n):
    return sorted(range(n), key=lambda d: -min(d, n - d))


def det_gather(det, full, sems, sent=lambda: None):
    send_sem, recv_sem, pass_send, pass_recv = sems
    me = lax.axis_index("det")
    others, partner = same_core(det)

    def copy(slot, to, a, b):
        return pltpu.make_async_remote_copy(
            src_ref=full.at[slot],
            dst_ref=full.at[slot],
            send_sem=a,
            recv_sem=b,
            device_id={"det": to},
            device_id_type=MESH,
        )

    n = det // 2
    order = sorted(range(1, n), key=lambda d: -min(d, n - d))
    outs = []
    for d in order:
        outs.append(copy(me, others[d - 1], send_sem.at[d], recv_sem.at[d]))
        outs[-1].start()
    outs.append(copy(me, partner, pass_send.at[0], pass_recv.at[0]))
    outs[-1].start()
    sent()
    for d in reversed(order):
        source = lax.rem(me + det - 2 * d, det)
        copy(source, me, send_sem.at[d], recv_sem.at[d]).wait_recv()
        outs.append(copy(source, partner, pass_send.at[d], pass_recv.at[d]))
        outs[-1].start()
    for d in range(n):
        source = lax.rem(partner + det - 2 * d, det)
        copy(source, partner, pass_send.at[d], pass_recv.at[d]).wait_recv()
    for out in outs:
        out.wait_send()


def pair_products(rows, along, k, transposed):
    dims = (((1,), (1 if transposed else 0,)), ((), ()))
    first = lax.dot_general(rows, along[k], dims, preferred_element_type=F32)
    second = lax.dot_general(rows, along[k + 1], dims, preferred_element_type=F32)
    index = lax.broadcasted_iota(jnp.int32, first.shape, 0)
    return jnp.where(index < MP, first, second)


def split_dot(exact, x, dims):
    high = x.astype(BF16)
    low = (x - high.astype(F32)).astype(BF16)
    dot = functools.partial(lax.dot_general, dimension_numbers=dims, preferred_element_type=F32)
    return dot(exact, high) + dot(exact, low)


ROWS_COLS = (((1,), (0,)), ((), ()))
COLS_COLS = (((0,), (0,)), ((), ()))


def place(slot_band, b):
    slot = slot_band.index(b)
    return slot // 2, (slot % 2) * FAST


def front_kernel(
    obs, det, grid, out_ref, pick_ref, along_ref, noise_ref, ke_ref, w_ref, fwd_ref, tw_ref, edge_ref, ends_ref,
    x_out, z_out, m_out,
    recv, fetched, scan, rows, other, ts, u, half, sums, e, es, payload, gathered, wide, zs, x,
    k0, k1, n0, n1, m0, m1, r0, r1, xs0, xs1, es0, es1, gs0, gs1, zs0, zs1, *sems,
):
    me, block = lax.axis_index("det"), lax.axis_index("obs")
    across, down = grid
    bx, by = block // down, lax.rem(block, down)
    n = det // 2
    chip, core, side = me // 2, lax.rem(me, 2), me // n
    dets, tiles = w_ref.shape[0], along_ref.shape[0]
    bands = [band_of(slot, det) for slot in range(det)]
    peers = all_det(det)
    greet(obs, det, True, peers)

    sky_start, sky_wait = obs_copies(obs, out_ref, recv, k0, k1)
    sky_start()
    part = noise_ref.shape[1] // 2
    whole = det_send(noise_ref, rows, n0.at[0], n1.at[0], lax.rem(2 * det - me, det))
    left = det_send(noise_ref.at[:, :part], other, n0.at[1], n1.at[1], det - 1 - me)
    right = det_send(noise_ref.at[:, part:], other, n0.at[1], n1.at[1], lax.rem(me + 1, det))

    @pl.when(core == 1)
    def _():
        whole.start()
        left.start()
        left.wait_send()
        whole.wait()

    @pl.when(core == 0)
    def _():
        right.start()
        rows[...] = noise_ref[...]
        right.wait_send()

    left.wait_recv()
    both = jnp.where(core == 1, rows[:, part:].astype(F32), rows[:, :part].astype(F32))
    m_out[bx, by] = (both + other[...].astype(F32)).astype(BF16)

    def sideways(d):
        to = lax.rem(bx + d, across)
        return pltpu.make_async_remote_copy(
            src_ref=m_out.at[bx, by],
            dst_ref=m_out.at[bx, by],
            send_sem=m0.at[d],
            recv_sem=m1.at[d],
            device_id={"obs": to * down + by},
            device_id_type=MESH,
        )

    def ring(way, step):
        origin = lax.rem(by + down - way * (step - 1), down)
        cut = slice(None)
        if 2 * step == down:
            cut = slice(0, across // 2) if way > 0 else slice(across // 2, across)
        at = 0 if way > 0 else 1
        return pltpu.make_async_remote_copy(
            src_ref=m_out.at[cut, origin],
            dst_ref=m_out.at[cut, origin],
            send_sem=r0.at[at, step - 1],
            recv_sem=r1.at[at, step - 1],
            device_id={"obs": bx * down + lax.rem(by + down + way, down)},
            device_id_type=MESH,
        )

    def turn(step):
        for way in (1, -1):
            if step == 1:
                if way == 1:
                    for d in range(1, across):
                        sideways(d).wait_recv()
            else:
                ring(way, step - 1).wait_recv()
            if 2 * step <= down:
                ring(way, step).start()

    steps = iter(range(1, down // 2 + 2))

    def advance():
        step = next(steps, None)
        if step is not None:
            turn(step)

    for d in range(1, across):
        sideways(d).start()

    sky_wait()
    flat = recv[...].reshape(obs * CAP * MP, LANES).astype(BF16)
    fetched[...] = jnp.dot(pick_ref[...], flat, preferred_element_type=F32).astype(BF16)
    for k in range(0, tiles, 4):
        part_rows = fetched[4 * k : 4 * k + 16]
        low = pair_products(part_rows[:8], along_ref, k, False)
        high = pair_products(part_rows[8:], along_ref, k + 2, False)
        scan[me, 4 * k : 4 * k + 16] = jnp.concatenate([low, high], 0).astype(BF16)
    det_gather(det, scan, sems, advance)

    for i in range(tiles // 4):
        rhs = scan[:, 16 * i : 16 * i + 16, :].reshape(det * 16, LANES)
        got = jnp.dot(ke_ref[...], rhs, preferred_element_type=F32)
        for q in range(4):
            k = 4 * i + q
            ts[k] = got[q * dets : (q + 1) * dets] * w_ref[:, k * LANES : (k + 1) * LANES].astype(F32)

    for h in range(2):

        def swap(g, carry):
            at = pl.ds(pl.multiple_of(g * 16, 16), 16)
            out = digit_swap([ts[h * det + i, at, :] for i in range(det)])
            for z in range(det):
                u[z, at, h * LANES : (h + 1) * LANES] = out[z].astype(BF16)
            return carry

        lax.fori_loop(0, dets // 16, swap, 0)

    sums[...] = jnp.zeros_like(sums)

    def ends(z, carry):
        sums[pl.ds(pl.multiple_of(z * 8, 8), 8), :dets] = lax.dot_general(
            ends_ref[...], u[z], (((1,), (1,)), ((), ())), preferred_element_type=F32
        )
        return carry

    lax.fori_loop(0, det, ends, 0)
    e[...] = split_dot(edge_ref[...], sums[...], ROWS_COLS)
    own = pl.ds(pl.multiple_of(me * 8, 8), 8)
    edges = []
    for d in range(1, det):
        to = peers[d - 1]
        edges.append(
            det_send(e.at[pl.ds(pl.multiple_of(to * 8, 8), 8)], es.at[own], es0.at[d], es1.at[d], to)
        )
        edges[-1].start()
    es[own, :] = e[own, :]
    advance()

    def fast(z, carry):
        a = jnp.dot(u[z], fwd_ref[...], preferred_element_type=F32)
        re, im = a[:, :LANES], a[:, LANES:]
        c, s = tw_ref[z, 0:1, :], tw_ref[z, 1:2, :]
        half[z, :, :LANES] = re * c + im * s
        half[z, :, LANES:] = im * c - re * s
        return carry

    lax.fori_loop(0, det, fast, 0)

    for copy in edges:
        copy.wait()
    for i in range(4):
        payload[16 * i : 16 * i + det] = es[pl.ds(i, det, stride=8), :].astype(BF16)
    give_start, give_wait = obs_copies(obs, payload, gathered, gs0, gs1, True)
    give_start()

    def last(g, carry):
        at = pl.ds(pl.multiple_of(g * 16, 16), 16)
        re = [half[z, at, :LANES] for z in range(det)]
        im = [half[z, at, LANES:] for z in range(det)]
        re, im = small_dft(re, im, -1)
        for b in range(det):
            to, lo = place(bands, b)
            x[to, at, lo : lo + LANES] = re[b].astype(BF16)
            x[to, at, lo + LANES : lo + FAST] = im[b].astype(BF16)
        return carry

    lax.fori_loop(0, dets // 16, last, 0)

    slot = lax.rem(me, n)

    def column(d):
        to = lax.rem(chip + d, n)
        return det_send(x.at[to], x_out.at[slot], xs0.at[d], xs1.at[slot], to * 2 + side)

    for d in far_first(n)[:-1]:
        column(d).start()
    mine = core == side

    @pl.when(mine)
    def _():
        x_out[slot] = x[chip]

    @pl.when(jnp.logical_not(mine))
    def _():
        column(0).start()

    advance()

    give_wait()
    wide[...] = gathered[...].reshape(obs * 64, LANES).astype(F32)
    width = noise_ref.shape[0]
    prod = jnp.zeros((obs * 4, width), F32)
    for j in range(det):
        lhs = wide[pl.ds(j, obs * 4, stride=16), :dets].astype(BF16)
        rhs = rows[:, j * dets : (j + 1) * dets]
        prod = prod + lax.dot_general(lhs, rhs, (((1,), (1,)), ((), ())), preferred_element_type=F32)
    zs[...] = jnp.zeros_like(zs)
    for p in range(obs):
        zs[p, 0:4, :width] = prod[4 * p : 4 * p + 4]
    z_start, z_wait = obs_copies(obs, zs, z_out, zs0, zs1)
    z_start()
    advance()
    advance()
    z_wait()

    for d in far_first(n)[:-1]:
        column(d).wait_send()

    @pl.when(jnp.logical_not(mine))
    def _():
        column(0).wait_send()

    for i in range(n):

        @pl.when(core * n + i != me)
        def _():
            det_send(x_out.at[i], x_out.at[i], xs0.at[0], xs1.at[i], me).wait_recv()

    for step in steps:
        turn(step)
    for d in range(1, across):
        sideways(d).wait_send()
    for step in range(1, down // 2 + 1):
        for way in (1, -1):
            ring(way, step).wait_send()


def all_det(det):
    me = lax.axis_index("det")
    return [lax.rem(me + d, det) for d in range(1, det)]


def det_send(src, dst, send_sem, recv_sem, to):
    return pltpu.make_async_remote_copy(
        src_ref=src,
        dst_ref=dst,
        send_sem=send_sem,
        recv_sem=recv_sem,
        device_id={"det": to},
        device_id_type=MESH,
    )


def far_first(n):
    return sorted(range(n), key=lambda d: -min(d, n - d))


def back_kernel(
    obs, det, m_ref, x_ref, z_ref, w_ref, ke_ref, inv_ref, tw_ref, edge_ref, ends_ref,
    along_ref, pick_ref, own_ref, sel_ref, sky_ref,
    given, taken, staged, y_ref, e_ref, turned, ts, sums, g_ref, pre, pairs, parts, total_ref, terms, leave, recv, full,
    ps0, ps1, ys0, ys1, fs0, fs1, g0, g1, q0, q1, s0, s1, *sems,
):
    me = lax.axis_index("det")
    n = det // 2
    chip, core = me // 2, lax.rem(me, 2)
    partner = me + 1 - 2 * core
    dets, tiles = w_ref.shape[0], along_ref.shape[0]
    bands = [band_of(slot, det) for slot in range(det)]
    slow = det
    peers = all_det(det)
    greet(obs, det, True, peers)
    per = obs // det
    finals = []
    for d in range(1, det):
        to = peers[d - 1]
        finals.append(det_send(z_ref.at[pl.ds(to * per, per)], e_ref.at[me], fs0.at[d], fs1.at[d], to))
        finals[-1].start()
    e_ref[me] = z_ref[pl.ds(me * per, per)]

    half = n // 2
    swaps, sends = [], []

    def product(to_chip):
        rows = m_ref[pl.ds(pl.multiple_of(to_chip * 2 * dets, 16), 2 * dets), :]
        return jnp.dot(rows, x_ref[...], preferred_element_type=F32)

    def finish(s, total):
        to_chip = core * half + lax.rem(chip + s, half)
        swaps[s].wait_recv()
        total = total + taken[s].astype(F32)
        for i in range(2):
            to = to_chip * 2 + i
            staged[s, i] = total[i * dets : (i + 1) * dets].astype(BF16)
            copy = det_send(staged.at[s, i], y_ref.at[chip], ys0.at[s, i], ys1.at[chip], to)

            @pl.when(to != me)
            def _():
                copy.start()

            @pl.when(to == me)
            def _():
                y_ref[chip] = staged[s, i]

            sends.append((to, copy))

    before = None
    for s in range(half):
        near = lax.rem(chip + s, half)
        given[s] = product((1 - core) * half + near).astype(BF16)
        swaps.append(det_send(given.at[s], taken.at[s], ps0.at[s], ps1.at[s], partner))
        swaps[-1].start()
        total = product(core * half + near)
        if before is not None:
            finish(s - 1, before)
        before = total
    finish(half - 1, before)
    side = me // n
    for c in range(n):

        @pl.when(c * 2 + side != me)
        def _():
            det_send(y_ref.at[c], y_ref.at[c], ys0.at[0, 0], ys1.at[c], me).wait_recv()

    for copy in swaps:
        copy.wait_send()
    for to, copy in sends:

        @pl.when(to != me)
        def _():
            copy.wait_send()
    for copy in finals:
        copy.wait()

    def first(g, carry):
        at = pl.ds(pl.multiple_of(g * 16, 16), 16)
        re, im = [], []
        for b in range(slow):
            chip, lo = place(bands, b)
            re.append(y_ref[chip, at, lo : lo + LANES].astype(F32))
            im.append(y_ref[chip, at, lo + LANES : lo + FAST].astype(F32))
        re, im = small_dft(re, im, 1)
        for z in range(slow):
            c, s = tw_ref[z, 0:1, :], tw_ref[z, 1:2, :]
            turned[z, at, :LANES] = (re[z] * c - im[z] * s).astype(BF16)
            turned[z, at, LANES:] = (im[z] * c + re[z] * s).astype(BF16)
        return carry

    lax.fori_loop(0, dets // 16, first, 0)
    part = dets // 2
    for q in range(2):
        rows = e_ref[:, q].reshape(8 * slow, LANES)
        sums[q] = split_dot(edge_ref[...], rows, COLS_COLS).astype(BF16).astype(F32)

    def fast(z, carry):
        o = jnp.dot(turned[z], inv_ref[...], preferred_element_type=F32)
        at = pl.ds(pl.multiple_of(z * 8, 8), 8)
        edge = [
            lax.dot_general(
                sums[q, at, :].astype(BF16), ends_ref[...], COLS_COLS, preferred_element_type=F32
            )[:part]
            for q in range(2)
        ]
        o = o + jnp.concatenate(edge, 0)
        ts[z] = o[:, :LANES]
        ts[slow + z] = o[:, LANES:]
        return carry

    lax.fori_loop(0, slow, fast, 0)

    for h in range(2):

        def swap(g, carry):
            at = pl.ds(pl.multiple_of(g * 16, 16), 16)
            out = digit_swap([ts[h * slow + z, at, :] for z in range(slow)])
            for i in range(slow):
                ts[h * slow + i, at, :] = out[i]
            return carry

        lax.fori_loop(0, dets // 16, swap, 0)

    for i in range(tiles // 4):
        filtered = [
            (ts[k] * w_ref[:, k * LANES : (k + 1) * LANES].astype(F32)).astype(BF16)
            for k in range(4 * i, 4 * i + 4)
        ]
        rows = lax.dot_general(
            ke_ref[...], jnp.concatenate(filtered, 0), COLS_COLS, preferred_element_type=F32
        )
        g_ref[:, :, 16 * i : 16 * i + 16, :] = rows.reshape(n, 2, 16, LANES).astype(BF16)

    swap_pairs = det_send(g_ref.at[:, 1 - core], pre, g0.at[0], g1.at[0], partner)
    swap_pairs.start()
    swap_pairs.wait()
    for c in range(n):
        pairs[c] = (g_ref[c, core].astype(F32) + pre[c].astype(F32)).astype(BF16)
    copies = []
    for d in far_first(n)[:-1]:
        to = lax.rem(chip + d, n)
        copies.append(det_send(pairs.at[to], parts.at[chip], q0.at[d], q1.at[d], to * 2 + core))
        copies[-1].start()
    parts[chip] = pairs[chip]
    for copy in copies:
        copy.wait()
    total = parts[0].astype(F32)
    for c in range(1, n):
        total = total + parts[c].astype(F32)
    total_ref[...] = total
    for k in range(0, tiles, 2):
        rows = total_ref[4 * k : 4 * k + 8]
        high = rows.astype(BF16)
        low = (rows - high.astype(F32)).astype(BF16)
        terms[4 * k : 4 * k + 8] = pair_products(high, along_ref, k, True) + pair_products(
            low, along_ref, k, True
        )
    leave[...] = split_dot(pick_ref[...], terms[...], COLS_COLS).reshape(obs, CAP * MP, LANES)
    start, wait = obs_copies(obs, leave, recv, s0, s1)
    start()
    wait()
    flat = recv[...].reshape(obs * CAP * MP, LANES)
    full[me] = split_dot(own_ref[...], flat, COLS_COLS).astype(BF16)
    det_gather(det, full, sems)
    held, rows_all = sky_ref.shape[0], sky_ref.shape[1]
    for i in range(held // 4):
        rhs = full[:, 16 * i : 16 * i + 16, :].reshape(det * 16, LANES)
        got = jnp.dot(sel_ref[...], rhs, preferred_element_type=F32)
        sky_ref[4 * i : 4 * i + 4] = got.reshape(4, rows_all, LANES)


def call(kernel, out, scratch, name, collective=None):
    if collective is None:
        params = pltpu.CompilerParams(vmem_limit_bytes=56 * 2**20)
    else:
        params = pltpu.CompilerParams(
            vmem_limit_bytes=56 * 2**20, collective_id=collective, has_side_effects=True
        )

    def run(*args):
        return pl.pallas_call(
            kernel,
            out_shape=out,
            in_specs=[VMEM] * len(args),
            out_specs=VMEM if not isinstance(out, tuple) else (VMEM,) * len(out),
            scratch_shapes=scratch,
            compiler_params=params,
            name=name,
        )(*args)

    return run


def dma(n):
    return [pltpu.SemaphoreType.DMA((n,))] * 2


def local(sky, tile_list, along, detector_kernel, sample_weight, noise_inverse):
    obs, det = lax.axis_size("obs"), lax.axis_size("det")
    me_obs, me_det = lax.axis_index("obs"), lax.axis_index("det")
    held, tiles = sky.shape[0], tile_list.shape[1]
    dets, all_dets = detector_kernel.shape[0], noise_inverse.shape[2]
    rows_all = sky.shape[1] * sky.shape[2]
    mine = rows_all // det
    fwd, inv, tw, edge, ends = tables(det)

    owner = tile_list // held
    earlier = jnp.arange(tiles)[None, :] < jnp.arange(tiles)[:, None]
    rank = jnp.sum(
        ((owner[:, :, None] == owner[:, None, :]) & earlier[None]).astype(jnp.int32), axis=2
    )
    slot_hit = (
        (owner == me_obs)[:, None, :] & (rank[:, None, :] == jnp.arange(CAP)[None, :, None])
    )
    inside = tile_list - me_obs * held
    wanted = jnp.max(jnp.where(slot_hit, inside[:, None, :] + 1, 0), axis=2) - 1
    wanted = jnp.broadcast_to(wanted[:, :, None], (obs, CAP, MP))
    row = jnp.arange(MP)[None, None, :]
    wanted = jnp.where(wanted >= 0, wanted * MP + row, -1).reshape(obs * CAP * MP, 1)
    own = (wanted == jnp.arange(held * MP)[None, :]).astype(BF16)
    slot = lax.dynamic_index_in_dim(owner * CAP + rank, me_obs, 0, keepdims=False)
    slot = (slot[:, None] * MP + jnp.arange(MP)[None, :]).reshape(tiles * MP, 1)
    pick = (slot == jnp.arange(obs * CAP * MP)[None, :]).astype(BF16)

    my_rows = lax.dynamic_slice_in_dim(sky.reshape(held, rows_all, LANES), me_det * mine, mine, 1)
    my_rows = jnp.pad(my_rows, ((0, 0), (0, MP - mine), (0, 0))).reshape(held * MP, LANES)
    outgoing = jnp.dot(own, my_rows, preferred_element_type=F32).reshape(obs, CAP * MP, LANES)

    wide = jnp.pad(detector_kernel.reshape(dets, det, mine), ((0, 0), (0, 0), (0, MP - mine)))
    ke = jnp.eye(4, dtype=BF16)[:, None, None, :, None] * wide[None, :, :, None, :]
    ke = ke.reshape(4 * dets, det * 16)
    sel = np.zeros((4, det, mine, det, 4, MP), np.float32)
    for q in range(4):
        for j in range(det):
            for m in range(mine):
                sel[q, j, m, j, q, m] = 1
    sel = jnp.asarray(sel.reshape(4 * rows_all, det * 16), BF16)

    block = along[0]
    n, half, per = det // 2, det // 4, obs // det
    down = 8 if obs == 32 else obs // 2
    grid = (obs // down, down)
    mine, part = noise_inverse.shape[1], all_dets // 2
    member = jax.ShapeDtypeStruct((n, dets, 2 * FAST), BF16)
    slots = jax.ShapeDtypeStruct((obs, CAP * MP, LANES), F32)
    slot_buffer = pltpu.VMEM(slots.shape, F32)
    row_buffer = pltpu.VMEM((tiles * MP, LANES), F32)
    banded, back, folded = call(
        functools.partial(front_kernel, obs, det, grid),
        (member, slots, jax.ShapeDtypeStruct((*grid, mine, part), BF16)),
        [
            slot_buffer,
            pltpu.VMEM((tiles * MP, LANES), BF16),
            pltpu.VMEM((det, tiles * MP, LANES), BF16),
            pltpu.VMEM((mine, all_dets), BF16),
            pltpu.VMEM((mine, part), BF16),
            pltpu.VMEM((tiles, dets, LANES), F32),
            pltpu.VMEM((det, dets, FAST), BF16),
            pltpu.VMEM((det, dets, FAST), F32),
            pltpu.VMEM((8 * det, LANES), F32),
            pltpu.VMEM((8 * det, LANES), F32),
            pltpu.VMEM((8 * det, LANES), F32),
            pltpu.VMEM((64, LANES), BF16),
            pltpu.VMEM((obs, 64, LANES), BF16),
            pltpu.VMEM((obs * 64, LANES), F32),
            slot_buffer,
            pltpu.VMEM(member.shape, BF16),
            *dma(obs),
            *dma(2),
            *dma(grid[0]),
            *[pltpu.SemaphoreType.DMA((2, down // 2))] * 2,
            *dma(n),
            *dma(det),
            *dma(obs),
            *dma(obs),
            *dma(n),
            *dma(n),
        ],
        "front",
        0,
    )(outgoing, pick, block, noise_inverse[0], ke, sample_weight, fwd, tw, edge, ends)
    normal = call(
        functools.partial(back_kernel, obs, det),
        jax.ShapeDtypeStruct((held, rows_all, LANES), F32),
        [
            pltpu.VMEM((half, 2 * dets, 2 * FAST), BF16),
            pltpu.VMEM((half, 2 * dets, 2 * FAST), BF16),
            pltpu.VMEM((half, 2, dets, 2 * FAST), BF16),
            pltpu.VMEM(member.shape, BF16),
            pltpu.VMEM((det, per, CAP * MP, LANES), F32),
            pltpu.VMEM((det, dets, FAST), BF16),
            pltpu.VMEM((tiles, dets, LANES), F32),
            pltpu.VMEM((2, 8 * det, LANES), F32),
            pltpu.VMEM((n, 2, tiles * MP, LANES), BF16),
            pltpu.VMEM((n, tiles * MP, LANES), BF16),
            pltpu.VMEM((n, tiles * MP, LANES), BF16),
            pltpu.VMEM((n, tiles * MP, LANES), BF16),
            row_buffer,
            row_buffer,
            slot_buffer,
            slot_buffer,
            pltpu.VMEM((det, held * MP, LANES), BF16),
            *dma(half),
            pltpu.SemaphoreType.DMA((half, 2)),
            pltpu.SemaphoreType.DMA((n,)),
            *dma(det),
            *dma(1),
            *dma(n),
            *dma(obs),
            *dma(n),
            *dma(n),
        ],
        "back",
        1,
    )(
        folded.reshape(all_dets, part), banded.reshape(n * dets, 2 * FAST), back,
        sample_weight, ke, inv, tw, edge, ends, block, pick, own, sel,
    )
    return normal.reshape(sky.shape)


def solution(mesh):
    in_specs = (
        P("obs", None, None, None),
        P(),
        P("obs", None, None, None),
        P("det", None),
        P("det", "obs"),
        P("det", "obs", None),
    )
    out_specs = P("obs", None, None, None)
    return jax.shard_map(local, mesh=mesh, in_specs=in_specs, out_specs=out_specs, check_vma=False)
```

time: 212 us -> 156 us (0.74)
  Pallas kernels: 188 us -> 145 us
  between operations: 13.5 us -> 0.1 us
    pallas_call x6 -> x2, Pallas kernels: 188 us -> 145 us  [run(): pl.pallas_call(kernel, out_shape=out, in_specs=[VMEM] * len(args), out_sp...]
  transfers between devices with their start and end apart: 1 -> 0, of which waited for: 0 -> 0; matrix products, arithmetic and copies ran while one was open for 4% -> 0% of each run, Pallas kernels for 41% -> 0%
where the time goes in v3:
time: 156 us
  Pallas kernels  145 us (93%)
  local copies, waits for them, and re-layouts  5.44 us (3%)
  other arithmetic  4.18 us (3%)
    pallas_call x2, Pallas kernels, run(): pl.pallas_call(kernel, out_shape=out, in_specs=[VMEM] * len(args), out_sp...  145 us

profile of v3, /device:TPU:1, one launch (start us, length us, event | category | flops | bytes accessed | tf_op | source)
XLA Modules:
  0.0 155.9 jit_solution(17991264481041987184)
XLA Ops:
  0.0 0.0 copy-start
  0.0 1.0 copy-done
  1.0 0.7 subtract_add_fusion
  1.7 0.7 reshape.133
  2.5 0.7 broadcast_compare_fusion
  3.2 0.8 convert_reduce_fusion
  4.0 0.1 select_reduce_fusion
  4.2 0.1 copy.18
  4.3 0.1 copy.19
  4.4 0.1 add_select_fusion
  4.5 0.1 select_n.37
  4.6 0.1 copy.20
  4.7 0.1 copy.21
  4.8 0.1 iota_add_fusion
  4.8 0.1 add.69
  5.0 0.7 fusion.4.own_ref
  5.8 0.7 fusion.3.pick_ref
  6.5 0.9 fusion.1.out_ref
  7.3 0.2 broadcast_multiply_fusion
  7.5 0.2 mul.62
  7.7 0.8 copy.22.ke_ref
  8.5 77.0 %front.1 = (bf16[8,96,512]{2,1,0:T(8,128)(2,1)}, f32[32,8,128]{2,1,0:T(8,128)}, bf16[4,8,48,768]{3,2,1,0:T(8,128)(2,1)}) custom-call(f32[32,8,128]{2,1,0:T(8,128)} %fusion.1.out_ref, bf16[128,256]{1,0:T(8,128)(2,1)} %fusion.3.pick_ref, bf16[32,128,128]{2,1,0:T(8,128)(2,1)} %bitcast.21, bf16[48,1536]{1,0:T(8,128)(2,1)} %bitcast.26, ...), custom_call_target="tpu_custom_call" | custom-call | tf_op jit(solution)/shard_map/front/pallas_call | solution.py:661
  85.5 68.3 %back.1 = f32[32,48,128]{2,1,0:T(8,128)} custom-call(bf16[1536,768]{1,0:T(8,128)(2,1)} %bitcast.24, bf16[768,512]{1,0:T(8,128)(2,1)} %bitcast.25, f32[32,8,128]{2,1,0:T(8,128)} %get-tuple-element.10.z_ref, bf16[96,4096]{1,0:T(8,128)(2,1)} %w_ref.3, bf16[384,256]{1,0:T(8,128)(2,1)} %copy.22.ke_ref, bf16[256,256]{1,0:T(8,128)(2,1)} %constant.62.clone.inv_ref, ...), custom_call_target="tpu_custom_call" | custom-call | tf_op jit(solution)/shard_map/back/pallas_call | solution.py:661
  153.8 2.1 %copy.25 = f32[32,3,16,128]{3,2,1,0:T(8,128)} copy(f32[32,3,16,128]{3,2,1,0:T(8,128)} %bitcast.23) | data formatting | bytes 1572864
  (7 shorter events, 0.1 us)
Async XLA Ops:
  0.0 1.0 copy-start

commit v4 on v3

--- a/solution.py
+++ b/solution.py
@@ -98,7 +98,7 @@
     return tiles
 
 
-def greet(obs, det, with_obs, det_peers):
+def greet(obs, det, with_obs, det_peers, meanwhile=None):
     barrier = pltpu.get_barrier_semaphore()
     count = 0
     if with_obs:
@@ -115,6 +115,8 @@
     for peer in det_peers:
         pl.semaphore_signal(barrier, inc=1, device_id={"det": peer}, device_id_type=MESH)
     count += len(det_peers)
+    if meanwhile is not None:
+        meanwhile()
     pl.semaphore_wait(barrier, count)
 
 
@@ -232,26 +234,94 @@
     return slot // 2, (slot % 2) * FAST
 
 
-def front_kernel(
-    obs, det, grid, out_ref, pick_ref, along_ref, noise_ref, ke_ref, w_ref, fwd_ref, tw_ref, edge_ref, ends_ref,
-    x_out, z_out, m_out,
-    recv, fetched, scan, rows, other, ts, u, half, sums, e, es, payload, gathered, wide, zs, x,
-    k0, k1, n0, n1, m0, m1, r0, r1, xs0, xs1, es0, es1, gs0, gs1, zs0, zs1, *sems,
+def all_det(det):
+    me = lax.axis_index("det")
+    return [lax.rem(me + d, det) for d in range(1, det)]
+
+
+def iota(shape, dim):
+    return lax.broadcasted_iota(jnp.int32, shape, dim)
+
+
+def selections(obs, list_ref, own, pick, mine_sel, mine, rows_all, held):
+    me, block = lax.axis_index("det"), lax.axis_index("obs")
+    tiles = list_ref.shape[1]
+    listed = list_ref[...]
+    owner = lax.div(listed, jnp.full_like(listed, held))
+    place_in = iota(listed.shape, 1).astype(F32)
+    hit = owner == block
+    inside = (listed - block * held + 1).astype(F32)
+    low = jnp.min(jnp.where(hit, place_in, F32(tiles)), 1, keepdims=True)
+    high = jnp.max(jnp.where(hit, place_in, F32(-1)), 1, keepdims=True)
+    first = jnp.where(hit & (place_in == low), inside, 0.0)
+    second = jnp.where(hit & (place_in == high) & (high > low), inside, 0.0)
+    size = obs * CAP * MP
+    wanted = jnp.full((size, LANES), -1.0, F32)
+    for s, found in enumerate((first, second)):
+        value = jnp.broadcast_to(jnp.sum(found, 1, keepdims=True), (obs, LANES)).astype(BF16)
+        row, col = iota((size, obs), 0), iota((size, obs), 1)
+        spread = (col == row // (CAP * MP)) & ((row // MP) % CAP == s)
+        wanted = wanted + jnp.dot(spread.astype(F32).astype(BF16), value, preferred_element_type=F32)
+    wide = (size, held * MP)
+    goal = wanted[:, : held * MP] * MP + (iota(wide, 0) % MP).astype(F32)
+    ok = (wanted[:, : held * MP] >= 0) & (goal == iota(wide, 1).astype(F32))
+    own[...] = ok.astype(F32).astype(BF16)
+    wide = (held * MP, held * rows_all)
+    row, col = iota(wide, 0), iota(wide, 1)
+    ok = (col == (row // MP) * rows_all + me * mine + row % MP) & (row % MP < mine)
+    mine_sel[...] = ok.astype(F32).astype(BF16)
+    owner = owner.astype(F32)
+    here = iota((obs, LANES), 0) == block
+    down = lax.dot_general(
+        owner.astype(BF16), here.astype(F32).astype(BF16), COLS_COLS, preferred_element_type=F32
+    )
+    along_row = jnp.sum(jnp.where(iota(listed.shape, 0) == block, owner, 0.0), 0, keepdims=True)
+    square = (tiles, tiles)
+    before = (down[:, :tiles] == along_row) & (iota(square, 1) < iota(square, 0))
+    rank = jnp.sum(before.astype(F32), 1, keepdims=True)
+    slot = (down * CAP + rank).astype(BF16)
+    tall = (tiles * MP, tiles)
+    spread = (iota(tall, 1) == iota(tall, 0) // MP).astype(F32).astype(BF16)
+    slot = jnp.dot(spread, slot, preferred_element_type=F32)
+    wide = (tiles * MP, size)
+    goal = jnp.broadcast_to(slot[:, :1], wide) * MP + (iota(wide, 0) % MP).astype(F32)
+    pick[...] = (goal == iota(wide, 1).astype(F32)).astype(F32).astype(BF16)
+
+
+def normal_kernel(
+    obs, det, grid, sky_in, list_ref, along_ref, noise_ref, kernel_ref, w_ref,
+    expand_ref, fwd_ref, inv_ref, tw_ref, edge_ref, ends_ref, sel_ref, sky_ref,
+    out_ref, own_ref, pick_ref, mine_sel, ke_ref, x_out, zz, m_out,
+    recv, fetched, scan, nrows, other, ts, u, spun, sums, e, es, payload, gathered, wide, zs, x,
+    given, taken, staged, y_ref, eb_ref, turned, esums, g_ref, pre, pairs, parts, total_ref, terms, leave, recv2, full,
+    k0, k1, n0, n1, m0, m1, r0, r1, xs0, xs1, es0, es1, gs0, gs1, zs0, zs1,
+    ps0, ps1, ys0, ys1, fs0, fs1, g0, g1, q0, q1, s0, s1, *sems,
 ):
     me, block = lax.axis_index("det"), lax.axis_index("obs")
     across, down = grid
     bx, by = block // down, lax.rem(block, down)
     n = det // 2
     chip, core, side = me // 2, lax.rem(me, 2), me // n
+    partner = me + 1 - 2 * core
     dets, tiles = w_ref.shape[0], along_ref.shape[0]
+    width = noise_ref.shape[0]
+    held, rows_all = sky_ref.shape[0], sky_ref.shape[1]
     bands = [band_of(slot, det) for slot in range(det)]
+    slow = det
     peers = all_det(det)
-    greet(obs, det, True, peers)
+
+    def prepare():
+        selections(obs, list_ref, own_ref, pick_ref, mine_sel, rows_all // det, rows_all, held)
+        my_rows = jnp.dot(mine_sel[...], sky_in[...], preferred_element_type=F32).astype(BF16)
+        got = jnp.dot(own_ref[...], my_rows, preferred_element_type=F32)
+        out_ref[...] = got.reshape(obs, CAP * MP, LANES)
+
+    greet(obs, det, True, peers, prepare)
 
     sky_start, sky_wait = obs_copies(obs, out_ref, recv, k0, k1)
     sky_start()
     part = noise_ref.shape[1] // 2
-    whole = det_send(noise_ref, rows, n0.at[0], n1.at[0], lax.rem(2 * det - me, det))
+    whole = det_send(noise_ref, nrows, n0.at[0], n1.at[0], lax.rem(2 * det - me, det))
     left = det_send(noise_ref.at[:, :part], other, n0.at[1], n1.at[1], det - 1 - me)
     right = det_send(noise_ref.at[:, part:], other, n0.at[1], n1.at[1], lax.rem(me + 1, det))
 
@@ -265,11 +335,11 @@
     @pl.when(core == 0)
     def _():
         right.start()
-        rows[...] = noise_ref[...]
+        nrows[...] = noise_ref[...]
         right.wait_send()
 
     left.wait_recv()
-    both = jnp.where(core == 1, rows[:, part:].astype(F32), rows[:, :part].astype(F32))
+    both = jnp.where(core == 1, nrows[:, part:].astype(F32), nrows[:, :part].astype(F32))
     m_out[bx, by] = (both + other[...].astype(F32)).astype(BF16)
 
     def sideways(d):
@@ -319,6 +389,12 @@
     for d in range(1, across):
         sideways(d).start()
 
+    for q in range(4):
+        cut = expand_ref[:, q * det * 16 : (q + 1) * det * 16]
+        ke_ref[q * dets : (q + 1) * dets] = jnp.dot(
+            kernel_ref[...], cut, preferred_element_type=F32
+        ).astype(BF16)
+
     sky_wait()
     flat = recv[...].reshape(obs * CAP * MP, LANES).astype(BF16)
     fetched[...] = jnp.dot(pick_ref[...], flat, preferred_element_type=F32).astype(BF16)
@@ -327,7 +403,7 @@
         low = pair_products(part_rows[:8], along_ref, k, False)
         high = pair_products(part_rows[8:], along_ref, k + 2, False)
         scan[me, 4 * k : 4 * k + 16] = jnp.concatenate([low, high], 0).astype(BF16)
-    det_gather(det, scan, sems, advance)
+    det_gather(det, scan, sems[:4], advance)
 
     for i in range(tiles // 4):
         rhs = scan[:, 16 * i : 16 * i + 16, :].reshape(det * 16, LANES)
@@ -372,8 +448,8 @@
         a = jnp.dot(u[z], fwd_ref[...], preferred_element_type=F32)
         re, im = a[:, :LANES], a[:, LANES:]
         c, s = tw_ref[z, 0:1, :], tw_ref[z, 1:2, :]
-        half[z, :, :LANES] = re * c + im * s
-        half[z, :, LANES:] = im * c - re * s
+        spun[z, :, :LANES] = re * c + im * s
+        spun[z, :, LANES:] = im * c - re * s
         return carry
 
     lax.fori_loop(0, det, fast, 0)
@@ -387,8 +463,8 @@
 
     def last(g, carry):
         at = pl.ds(pl.multiple_of(g * 16, 16), 16)
-        re = [half[z, at, :LANES] for z in range(det)]
-        im = [half[z, at, LANES:] for z in range(det)]
+        re = [spun[z, at, :LANES] for z in range(det)]
+        im = [spun[z, at, LANES:] for z in range(det)]
         re, im = small_dft(re, im, -1)
         for b in range(det):
             to, lo = place(bands, b)
@@ -418,30 +494,7 @@
 
     advance()
 
-    give_wait()
-    wide[...] = gathered[...].reshape(obs * 64, LANES).astype(F32)
-    width = noise_ref.shape[0]
-    prod = jnp.zeros((obs * 4, width), F32)
-    for j in range(det):
-        lhs = wide[pl.ds(j, obs * 4, stride=16), :dets].astype(BF16)
-        rhs = rows[:, j * dets : (j + 1) * dets]
-        prod = prod + lax.dot_general(lhs, rhs, (((1,), (1,)), ((), ())), preferred_element_type=F32)
-    zs[...] = jnp.zeros_like(zs)
-    for p in range(obs):
-        zs[p, 0:4, :width] = prod[4 * p : 4 * p + 4]
-    z_start, z_wait = obs_copies(obs, zs, z_out, zs0, zs1)
-    z_start()
     advance()
-    advance()
-    z_wait()
-
-    for d in far_first(n)[:-1]:
-        column(d).wait_send()
-
-    @pl.when(jnp.logical_not(mine))
-    def _():
-        column(0).wait_send()
-
     for i in range(n):
 
         @pl.when(core * n + i != me)
@@ -450,65 +503,18 @@
 
     for step in steps:
         turn(step)
-    for d in range(1, across):
-        sideways(d).wait_send()
-    for step in range(1, down // 2 + 1):
-        for way in (1, -1):
-            ring(way, step).wait_send()
-
-
-def all_det(det):
-    me = lax.axis_index("det")
-    return [lax.rem(me + d, det) for d in range(1, det)]
-
-
-def det_send(src, dst, send_sem, recv_sem, to):
-    return pltpu.make_async_remote_copy(
-        src_ref=src,
-        dst_ref=dst,
-        send_sem=send_sem,
-        recv_sem=recv_sem,
-        device_id={"det": to},
-        device_id_type=MESH,
-    )
-
-
-def far_first(n):
-    return sorted(range(n), key=lambda d: -min(d, n - d))
-
-
-def back_kernel(
-    obs, det, m_ref, x_ref, z_ref, w_ref, ke_ref, inv_ref, tw_ref, edge_ref, ends_ref,
-    along_ref, pick_ref, own_ref, sel_ref, sky_ref,
-    given, taken, staged, y_ref, e_ref, turned, ts, sums, g_ref, pre, pairs, parts, total_ref, terms, leave, recv, full,
-    ps0, ps1, ys0, ys1, fs0, fs1, g0, g1, q0, q1, s0, s1, *sems,
-):
-    me = lax.axis_index("det")
-    n = det // 2
-    chip, core = me // 2, lax.rem(me, 2)
-    partner = me + 1 - 2 * core
-    dets, tiles = w_ref.shape[0], along_ref.shape[0]
-    bands = [band_of(slot, det) for slot in range(det)]
-    slow = det
-    peers = all_det(det)
-    greet(obs, det, True, peers)
-    per = obs // det
-    finals = []
-    for d in range(1, det):
-        to = peers[d - 1]
-        finals.append(det_send(z_ref.at[pl.ds(to * per, per)], e_ref.at[me], fs0.at[d], fs1.at[d], to))
-        finals[-1].start()
-    e_ref[me] = z_ref[pl.ds(me * per, per)]
-
-    half = n // 2
+
+    hn = n // 2
     swaps, sends = [], []
 
     def product(to_chip):
-        rows = m_ref[pl.ds(pl.multiple_of(to_chip * 2 * dets, 16), 2 * dets), :]
-        return jnp.dot(rows, x_ref[...], preferred_element_type=F32)
+        at = to_chip * (2 * dets // width)
+        rows = m_out[at // down, pl.ds(lax.rem(at, down), 2 * dets // width)]
+        rows = rows.reshape(2 * dets, m_out.shape[3])
+        return jnp.dot(rows, x_out[...].reshape(n * dets, 2 * FAST), preferred_element_type=F32)
 
     def finish(s, total):
-        to_chip = core * half + lax.rem(chip + s, half)
+        to_chip = core * hn + lax.rem(chip + s, hn)
         swaps[s].wait_recv()
         total = total + taken[s].astype(F32)
         for i in range(2):
@@ -527,30 +533,43 @@
             sends.append((to, copy))
 
     before = None
-    for s in range(half):
-        near = lax.rem(chip + s, half)
-        given[s] = product((1 - core) * half + near).astype(BF16)
+    for s in range(hn):
+        near = lax.rem(chip + s, hn)
+        given[s] = product((1 - core) * hn + near).astype(BF16)
         swaps.append(det_send(given.at[s], taken.at[s], ps0.at[s], ps1.at[s], partner))
         swaps[-1].start()
-        total = product(core * half + near)
+        total = product(core * hn + near)
         if before is not None:
             finish(s - 1, before)
         before = total
-    finish(half - 1, before)
-    side = me // n
+    finish(hn - 1, before)
+    give_wait()
+    wide[...] = gathered[...].reshape(obs * 64, LANES).astype(F32)
+    prod = jnp.zeros((obs * 4, width), F32)
+    for j in range(det):
+        lhs = wide[pl.ds(j, obs * 4, stride=16), :dets].astype(BF16)
+        rhs = nrows[:, j * dets : (j + 1) * dets]
+        prod = prod + lax.dot_general(lhs, rhs, (((1,), (1,)), ((), ())), preferred_element_type=F32)
+    zs[...] = jnp.zeros_like(zs)
+    for p in range(obs):
+        zs[p, 0:4, :width] = prod[4 * p : 4 * p + 4]
+    z_start, z_wait = obs_copies(obs, zs, zz, zs0, zs1)
+    z_start()
+    z_wait()
+    per = obs // det
+    finals = []
+    for d in range(1, det):
+        to = peers[d - 1]
+        finals.append(det_send(zz.at[pl.ds(to * per, per)], eb_ref.at[me], fs0.at[d], fs1.at[d], to))
+        finals[-1].start()
+    eb_ref[me] = zz[pl.ds(me * per, per)]
+
     for c in range(n):
 
         @pl.when(c * 2 + side != me)
         def _():
             det_send(y_ref.at[c], y_ref.at[c], ys0.at[0, 0], ys1.at[c], me).wait_recv()
 
-    for copy in swaps:
-        copy.wait_send()
-    for to, copy in sends:
-
-        @pl.when(to != me)
-        def _():
-            copy.wait_send()
     for copy in finals:
         copy.wait()
 
@@ -569,18 +588,17 @@
         return carry
 
     lax.fori_loop(0, dets // 16, first, 0)
-    part = dets // 2
     for q in range(2):
-        rows = e_ref[:, q].reshape(8 * slow, LANES)
-        sums[q] = split_dot(edge_ref[...], rows, COLS_COLS).astype(BF16).astype(F32)
+        rows = eb_ref[:, q].reshape(8 * slow, LANES)
+        esums[q] = split_dot(edge_ref[...], rows, COLS_COLS).astype(BF16).astype(F32)
 
     def fast(z, carry):
         o = jnp.dot(turned[z], inv_ref[...], preferred_element_type=F32)
         at = pl.ds(pl.multiple_of(z * 8, 8), 8)
         edge = [
             lax.dot_general(
-                sums[q, at, :].astype(BF16), ends_ref[...], COLS_COLS, preferred_element_type=F32
-            )[:part]
+                esums[q, at, :].astype(BF16), ends_ref[...], COLS_COLS, preferred_element_type=F32
+            )[: dets // 2]
             for q in range(2)
         ]
         o = o + jnp.concatenate(edge, 0)
@@ -636,17 +654,36 @@
             low, along_ref, k, True
         )
     leave[...] = split_dot(pick_ref[...], terms[...], COLS_COLS).reshape(obs, CAP * MP, LANES)
-    start, wait = obs_copies(obs, leave, recv, s0, s1)
+    start, wait = obs_copies(obs, leave, recv2, s0, s1)
     start()
     wait()
-    flat = recv[...].reshape(obs * CAP * MP, LANES)
+    flat = recv2[...].reshape(obs * CAP * MP, LANES)
     full[me] = split_dot(own_ref[...], flat, COLS_COLS).astype(BF16)
-    det_gather(det, full, sems)
-    held, rows_all = sky_ref.shape[0], sky_ref.shape[1]
+    det_gather(det, full, sems[4:])
     for i in range(held // 4):
         rhs = full[:, 16 * i : 16 * i + 16, :].reshape(det * 16, LANES)
         got = jnp.dot(sel_ref[...], rhs, preferred_element_type=F32)
         sky_ref[4 * i : 4 * i + 4] = got.reshape(4, rows_all, LANES)
+    for copy in swaps:
+        copy.wait_send()
+    for to, copy in sends:
+
+        @pl.when(to != me)
+        def _():
+            copy.wait_send()
+
+    for d in far_first(n)[:-1]:
+        column(d).wait_send()
+
+    @pl.when(jnp.logical_not(mine))
+    def _():
+        column(0).wait_send()
+
+    for d in range(1, across):
+        sideways(d).wait_send()
+    for step in range(1, down // 2 + 1):
+        for way in (1, -1):
+            ring(way, step).wait_send()
 
 
 def call(kernel, out, scratch, name, collective=None):
@@ -677,38 +714,18 @@
 
 def local(sky, tile_list, along, detector_kernel, sample_weight, noise_inverse):
     obs, det = lax.axis_size("obs"), lax.axis_size("det")
-    me_obs, me_det = lax.axis_index("obs"), lax.axis_index("det")
     held, tiles = sky.shape[0], tile_list.shape[1]
     dets, all_dets = detector_kernel.shape[0], noise_inverse.shape[2]
     rows_all = sky.shape[1] * sky.shape[2]
     mine = rows_all // det
     fwd, inv, tw, edge, ends = tables(det)
 
-    owner = tile_list // held
-    earlier = jnp.arange(tiles)[None, :] < jnp.arange(tiles)[:, None]
-    rank = jnp.sum(
-        ((owner[:, :, None] == owner[:, None, :]) & earlier[None]).astype(jnp.int32), axis=2
-    )
-    slot_hit = (
-        (owner == me_obs)[:, None, :] & (rank[:, None, :] == jnp.arange(CAP)[None, :, None])
-    )
-    inside = tile_list - me_obs * held
-    wanted = jnp.max(jnp.where(slot_hit, inside[:, None, :] + 1, 0), axis=2) - 1
-    wanted = jnp.broadcast_to(wanted[:, :, None], (obs, CAP, MP))
-    row = jnp.arange(MP)[None, None, :]
-    wanted = jnp.where(wanted >= 0, wanted * MP + row, -1).reshape(obs * CAP * MP, 1)
-    own = (wanted == jnp.arange(held * MP)[None, :]).astype(BF16)
-    slot = lax.dynamic_index_in_dim(owner * CAP + rank, me_obs, 0, keepdims=False)
-    slot = (slot[:, None] * MP + jnp.arange(MP)[None, :]).reshape(tiles * MP, 1)
-    pick = (slot == jnp.arange(obs * CAP * MP)[None, :]).astype(BF16)
-
-    my_rows = lax.dynamic_slice_in_dim(sky.reshape(held, rows_all, LANES), me_det * mine, mine, 1)
-    my_rows = jnp.pad(my_rows, ((0, 0), (0, MP - mine), (0, 0))).reshape(held * MP, LANES)
-    outgoing = jnp.dot(own, my_rows, preferred_element_type=F32).reshape(obs, CAP * MP, LANES)
-
-    wide = jnp.pad(detector_kernel.reshape(dets, det, mine), ((0, 0), (0, 0), (0, MP - mine)))
-    ke = jnp.eye(4, dtype=BF16)[:, None, None, :, None] * wide[None, :, :, None, :]
-    ke = ke.reshape(4 * dets, det * 16)
+    expand = np.zeros((rows_all, 4, det, 4, MP), np.float32)
+    for q in range(4):
+        for j in range(det):
+            for m in range(mine):
+                expand[j * mine + m, q, j, q, m] = 1
+    expand = jnp.asarray(expand.reshape(rows_all, -1), BF16)
     sel = np.zeros((4, det, mine, det, 4, MP), np.float32)
     for q in range(4):
         for j in range(det):
@@ -725,10 +742,21 @@
     slots = jax.ShapeDtypeStruct((obs, CAP * MP, LANES), F32)
     slot_buffer = pltpu.VMEM(slots.shape, F32)
     row_buffer = pltpu.VMEM((tiles * MP, LANES), F32)
-    banded, back, folded = call(
-        functools.partial(front_kernel, obs, det, grid),
-        (member, slots, jax.ShapeDtypeStruct((*grid, mine, part), BF16)),
+    pieces = pltpu.VMEM((n, tiles * MP, LANES), BF16)
+    edge_rows = pltpu.VMEM((8 * det, LANES), F32)
+    mixed = pltpu.VMEM((half, 2 * dets, 2 * FAST), BF16)
+    normal = call(
+        functools.partial(normal_kernel, obs, det, grid),
+        jax.ShapeDtypeStruct((held, rows_all, LANES), F32),
         [
+            slot_buffer,
+            pltpu.VMEM((obs * CAP * MP, held * MP), BF16),
+            pltpu.VMEM((tiles * MP, obs * CAP * MP), BF16),
+            pltpu.VMEM((held * MP, held * rows_all), BF16),
+            pltpu.VMEM((4 * dets, det * 16), BF16),
+            pltpu.VMEM(member.shape, BF16),
+            slot_buffer,
+            pltpu.VMEM((*grid, mine, part), BF16),
             slot_buffer,
             pltpu.VMEM((tiles * MP, LANES), BF16),
             pltpu.VMEM((det, tiles * MP, LANES), BF16),
@@ -737,14 +765,30 @@
             pltpu.VMEM((tiles, dets, LANES), F32),
             pltpu.VMEM((det, dets, FAST), BF16),
             pltpu.VMEM((det, dets, FAST), F32),
-            pltpu.VMEM((8 * det, LANES), F32),
-            pltpu.VMEM((8 * det, LANES), F32),
-            pltpu.VMEM((8 * det, LANES), F32),
+            edge_rows,
+            edge_rows,
+            edge_rows,
             pltpu.VMEM((64, LANES), BF16),
             pltpu.VMEM((obs, 64, LANES), BF16),
             pltpu.VMEM((obs * 64, LANES), F32),
             slot_buffer,
             pltpu.VMEM(member.shape, BF16),
+            mixed,
+            mixed,
+            pltpu.VMEM((half, 2, dets, 2 * FAST), BF16),
+            pltpu.VMEM(member.shape, BF16),
+            pltpu.VMEM((det, per, CAP * MP, LANES), F32),
+            pltpu.VMEM((det, dets, FAST), BF16),
+            pltpu.VMEM((2, 8 * det, LANES), F32),
+            pltpu.VMEM((n, 2, tiles * MP, LANES), BF16),
+            pieces,
+            pieces,
+            pieces,
+            row_buffer,
+            row_buffer,
+            slot_buffer,
+            slot_buffer,
+            pltpu.VMEM((det, held * MP, LANES), BF16),
             *dma(obs),
             *dma(2),
             *dma(grid[0]),
@@ -753,33 +797,6 @@
             *dma(det),
             *dma(obs),
             *dma(obs),
-            *dma(n),
-            *dma(n),
-        ],
-        "front",
-        0,
-    )(outgoing, pick, block, noise_inverse[0], ke, sample_weight, fwd, tw, edge, ends)
-    normal = call(
-        functools.partial(back_kernel, obs, det),
-        jax.ShapeDtypeStruct((held, rows_all, LANES), F32),
-        [
-            pltpu.VMEM((half, 2 * dets, 2 * FAST), BF16),
-            pltpu.VMEM((half, 2 * dets, 2 * FAST), BF16),
-            pltpu.VMEM((half, 2, dets, 2 * FAST), BF16),
-            pltpu.VMEM(member.shape, BF16),
-            pltpu.VMEM((det, per, CAP * MP, LANES), F32),
-            pltpu.VMEM((det, dets, FAST), BF16),
-            pltpu.VMEM((tiles, dets, LANES), F32),
-            pltpu.VMEM((2, 8 * det, LANES), F32),
-            pltpu.VMEM((n, 2, tiles * MP, LANES), BF16),
-            pltpu.VMEM((n, tiles * MP, LANES), BF16),
-            pltpu.VMEM((n, tiles * MP, LANES), BF16),
-            pltpu.VMEM((n, tiles * MP, LANES), BF16),
-            row_buffer,
-            row_buffer,
-            slot_buffer,
-            slot_buffer,
-            pltpu.VMEM((det, held * MP, LANES), BF16),
             *dma(half),
             pltpu.SemaphoreType.DMA((half, 2)),
             pltpu.SemaphoreType.DMA((n,)),
@@ -789,12 +806,14 @@
             *dma(obs),
             *dma(n),
             *dma(n),
+            *dma(n),
+            *dma(n),
         ],
-        "back",
-        1,
+        "normal",
+        0,
     )(
-        folded.reshape(all_dets, part), banded.reshape(n * dets, 2 * FAST), back,
-        sample_weight, ke, inv, tw, edge, ends, block, pick, own, sel,
+        sky.reshape(held * rows_all, LANES), tile_list, block, noise_inverse[0], detector_kernel, sample_weight,
+        expand, fwd, inv, tw, edge, ends, sel,
     )
     return normal.reshape(sky.shape)
 

time: 156 us -> 142 us (0.910)
  Pallas kernels: 145 us -> 139 us
  other arithmetic: 4.18 us -> 0 us
  local copies, waits for them, and re-layouts: 5.44 us -> 3.47 us
    pallas_call x2 -> x1, Pallas kernels: 145 us -> 139 us  [run(): pl.pallas_call(kernel, out_shape=out, in_specs=[VMEM] * len(args), out_sp...]
    unnamed x3 -> x2, local copies, waits for them, and re-layouts: 3.06 us -> 3.47 us
where the time goes in v4:
time: 142 us
  Pallas kernels  139 us (98%)
  local copies, waits for them, and re-layouts  3.47 us (2%)
    pallas_call x1, Pallas kernels, run(): pl.pallas_call(kernel, out_shape=out, in_specs=[VMEM] * len(args), out_sp...  139 us
    unnamed x2, local copies, waits for them, and re-layouts  3.47 us

profile of v4, /device:TPU:1, one launch (start us, length us, event | category | flops | bytes accessed | tf_op | source)
XLA Modules:
  0.0 142.1 jit_solution(15783922046690357273)
XLA Ops:
  0.0 1.4 copy.14.kernel_ref
  1.4 138.6 %normal.1 = f32[32,48,128]{2,1,0:T(8,128)} custom-call(bf16[1536,128]{1,0:T(8,128)(2,1)} %bitcast.6, s32[32,32]{1,0:T(8,128)} %list_ref.1, bf16[32,128,128]{2,1,0:T(8,128)(2,1)} %bitcast.5, bf16[48,1536]{1,0:T(8,128)(2,1)} %bitcast.7, bf16[96,48]{1,0:T(8,128)(2,1)} %copy.14.kernel_ref, bf16[96,4096]{1,0:T(8,128)(2,1)} %w_ref.1, ...), custom_call_target="tpu_custom_call" | custom-call | tf_op jit(solution)/shard_map/normal/pallas_call | solution.py:698
  140.1 2.1 %copy.16 = f32[32,3,16,128]{3,2,1,0:T(8,128)} copy(f32[32,3,16,128]{3,2,1,0:T(8,128)} %bitcast.4) | data formatting | bytes 1572864

commit v5 on v4

--- a/solution.py
+++ b/solution.py
@@ -293,9 +293,9 @@
     expand_ref, fwd_ref, inv_ref, tw_ref, edge_ref, ends_ref, sel_ref, sky_ref,
     out_ref, own_ref, pick_ref, mine_sel, ke_ref, x_out, zz, m_out,
     recv, fetched, scan, nrows, other, ts, u, spun, sums, e, es, payload, gathered, wide, zs, x,
-    given, taken, staged, y_ref, eb_ref, turned, esums, g_ref, pre, pairs, parts, total_ref, terms, leave, recv2, full,
+    given, taken, staged, y_ref, eb_ref, turned, esums, g_ref, pre, pairs, parts, total_ref, terms, leave, recv2, full, by_x, by_y,
     k0, k1, n0, n1, m0, m1, r0, r1, xs0, xs1, es0, es1, gs0, gs1, zs0, zs1,
-    ps0, ps1, ys0, ys1, fs0, fs1, g0, g1, q0, q1, s0, s1, *sems,
+    ps0, ps1, ys0, ys1, vx0, vx1, wx0, vy0, vy1, wy0, fs0, fs1, g0, g1, q0, q1, s0, s1, *sems,
 ):
     me, block = lax.axis_index("det"), lax.axis_index("obs")
     across, down = grid
@@ -405,23 +405,103 @@
         scan[me, 4 * k : 4 * k + 16] = jnp.concatenate([low, high], 0).astype(BF16)
     det_gather(det, scan, sems[:4], advance)
 
-    for i in range(tiles // 4):
-        rhs = scan[:, 16 * i : 16 * i + 16, :].reshape(det * 16, LANES)
-        got = jnp.dot(ke_ref[...], rhs, preferred_element_type=F32)
-        for q in range(4):
-            k = 4 * i + q
-            ts[k] = got[q * dets : (q + 1) * dets] * w_ref[:, k * LANES : (k + 1) * LANES].astype(F32)
-
-    for h in range(2):
-
-        def swap(g, carry):
-            at = pl.ds(pl.multiple_of(g * 16, 16), 16)
-            out = digit_swap([ts[h * det + i, at, :] for i in range(det)])
-            for z in range(det):
-                u[z, at, h * LANES : (h + 1) * LANES] = out[z].astype(BF16)
+    chunk = dets // 2
+    cuts = [slice(c * chunk, (c + 1) * chunk) for c in range(2)]
+    far = n // 2
+    relayed = n >= 4
+    slot = lax.rem(me, n)
+    back_chip = lax.rem(chip + n - 1, n)
+    from_chip = lax.rem(chip + 1, n)
+    from_side = from_chip // far
+    final_chip = lax.rem(from_chip + far, n)
+    mine = core == side
+    lefts = []
+
+    def column(d, c):
+        to = lax.rem(chip + d, n)
+        return det_send(
+            x.at[to, cuts[c]], x_out.at[slot, cuts[c]], xs0.at[d, c], xs1.at[slot, c], to * 2 + side
+        )
+
+    def over(source):
+        to = back_chip * 2 + side
+        return det_send(x.at[lax.rem(chip + far, n), cuts[0]], by_x.at[source], vx0.at[0], vx1.at[source], to)
+
+    def onward(source):
+        at = lax.rem(from_chip * 2 + source, n)
+        return det_send(
+            by_x.at[source], x_out.at[at, cuts[0]], wx0.at[source], xs1.at[at, 0], final_chip * 2 + from_side
+        )
+
+    def timestream(c):
+        for i in range(tiles // 4):
+            rhs = scan[:, 16 * i : 16 * i + 16, :].reshape(det * 16, LANES)
+            lhs = [ke_ref[q * dets + c * chunk : q * dets + (c + 1) * chunk] for q in range(4)]
+            got = jnp.dot(jnp.concatenate(lhs, 0), rhs, preferred_element_type=F32)
+            for q in range(4):
+                k = 4 * i + q
+                weight = w_ref[cuts[c], k * LANES : (k + 1) * LANES].astype(F32)
+                ts[k, cuts[c]] = got[q * chunk : (q + 1) * chunk] * weight
+        for h in range(2):
+
+            def swap(g, carry):
+                at = pl.ds(pl.multiple_of(c * chunk + g * 16, 16), 16)
+                out = digit_swap([ts[h * det + i, at, :] for i in range(det)])
+                for z in range(det):
+                    u[z, at, h * LANES : (h + 1) * LANES] = out[z].astype(BF16)
+                return carry
+
+            lax.fori_loop(0, chunk // 16, swap, 0)
+
+    def transform(c):
+        def fast(z, carry):
+            a = jnp.dot(u[z, cuts[c]], fwd_ref[...], preferred_element_type=F32)
+            re, im = a[:, :LANES], a[:, LANES:]
+            cs, sn = tw_ref[z, 0:1, :], tw_ref[z, 1:2, :]
+            spun[z, cuts[c], :LANES] = re * cs + im * sn
+            spun[z, cuts[c], LANES:] = im * cs - re * sn
             return carry
 
-        lax.fori_loop(0, dets // 16, swap, 0)
+        lax.fori_loop(0, det, fast, 0)
+
+        def last(g, carry):
+            at = pl.ds(pl.multiple_of(c * chunk + g * 16, 16), 16)
+            re = [spun[z, at, :LANES] for z in range(det)]
+            im = [spun[z, at, LANES:] for z in range(det)]
+            re, im = small_dft(re, im, -1)
+            for b in range(det):
+                to, lo = place(bands, b)
+                x[to, at, lo : lo + LANES] = re[b].astype(BF16)
+                x[to, at, lo + LANES : lo + FAST] = im[b].astype(BF16)
+            return carry
+
+        lax.fori_loop(0, chunk // 16, last, 0)
+
+    def send_columns(c):
+        for d in far_first(n)[:-1]:
+            if relayed and c == 0 and d == far:
+                for source in range(2):
+
+                    @pl.when(core == source)
+                    def _():
+                        over(source).start()
+            else:
+                column(d, c).start()
+                lefts.append(column(d, c))
+
+        @pl.when(mine)
+        def _():
+            x_out[slot, cuts[c]] = x[chip, cuts[c]]
+
+        @pl.when(jnp.logical_not(mine))
+        def _():
+            column(0, c).start()
+
+    timestream(0)
+    transform(0)
+    send_columns(0)
+    advance()
+    timestream(1)
 
     sums[...] = jnp.zeros_like(sums)
 
@@ -430,6 +510,17 @@
             ends_ref[...], u[z], (((1,), (1,)), ((), ())), preferred_element_type=F32
         )
         return carry
+
+    transform(1)
+    send_columns(1)
+    advance()
+    if relayed:
+
+        @pl.when(core == from_side)
+        def _():
+            for source in range(2):
+                det_send(by_x.at[source], by_x.at[source], vx0.at[0], vx1.at[source], me).wait_recv()
+                onward(source).start()
 
     lax.fori_loop(0, det, ends, 0)
     e[...] = split_dot(edge_ref[...], sums[...], ROWS_COLS)
@@ -443,63 +534,21 @@
         edges[-1].start()
     es[own, :] = e[own, :]
     advance()
-
-    def fast(z, carry):
-        a = jnp.dot(u[z], fwd_ref[...], preferred_element_type=F32)
-        re, im = a[:, :LANES], a[:, LANES:]
-        c, s = tw_ref[z, 0:1, :], tw_ref[z, 1:2, :]
-        spun[z, :, :LANES] = re * c + im * s
-        spun[z, :, LANES:] = im * c - re * s
-        return carry
-
-    lax.fori_loop(0, det, fast, 0)
-
     for copy in edges:
         copy.wait()
     for i in range(4):
         payload[16 * i : 16 * i + det] = es[pl.ds(i, det, stride=8), :].astype(BF16)
     give_start, give_wait = obs_copies(obs, payload, gathered, gs0, gs1, True)
     give_start()
-
-    def last(g, carry):
-        at = pl.ds(pl.multiple_of(g * 16, 16), 16)
-        re = [spun[z, at, :LANES] for z in range(det)]
-        im = [spun[z, at, LANES:] for z in range(det)]
-        re, im = small_dft(re, im, -1)
-        for b in range(det):
-            to, lo = place(bands, b)
-            x[to, at, lo : lo + LANES] = re[b].astype(BF16)
-            x[to, at, lo + LANES : lo + FAST] = im[b].astype(BF16)
-        return carry
-
-    lax.fori_loop(0, dets // 16, last, 0)
-
-    slot = lax.rem(me, n)
-
-    def column(d):
-        to = lax.rem(chip + d, n)
-        return det_send(x.at[to], x_out.at[slot], xs0.at[d], xs1.at[slot], to * 2 + side)
-
-    for d in far_first(n)[:-1]:
-        column(d).start()
-    mine = core == side
-
-    @pl.when(mine)
-    def _():
-        x_out[slot] = x[chip]
-
-    @pl.when(jnp.logical_not(mine))
-    def _():
-        column(0).start()
-
-    advance()
-
     advance()
     for i in range(n):
 
         @pl.when(core * n + i != me)
         def _():
-            det_send(x_out.at[i], x_out.at[i], xs0.at[0], xs1.at[i], me).wait_recv()
+            for c in range(2):
+                det_send(
+                    x_out.at[i, cuts[c]], x_out.at[i, cuts[c]], xs0.at[0, c], xs1.at[i, c], me
+                ).wait_recv()
 
     for step in steps:
         turn(step)
@@ -507,42 +556,65 @@
     hn = n // 2
     swaps, sends = [], []
 
-    def product(to_chip):
-        at = to_chip * (2 * dets // width)
-        rows = m_out[at // down, pl.ds(lax.rem(at, down), 2 * dets // width)]
-        rows = rows.reshape(2 * dets, m_out.shape[3])
+    def product(to_chip, c):
+        blocks = [to_chip * 4 + 2 * i + c for i in range(2)]
+        rows = jnp.concatenate([m_out[at // down, lax.rem(at, down)] for at in blocks], 0)
         return jnp.dot(rows, x_out[...].reshape(n * dets, 2 * FAST), preferred_element_type=F32)
 
-    def finish(s, total):
+    def finish(c, s, total):
         to_chip = core * hn + lax.rem(chip + s, hn)
-        swaps[s].wait_recv()
-        total = total + taken[s].astype(F32)
+        swaps[c * hn + s].wait_recv()
+        total = total + taken[c, s].astype(F32)
         for i in range(2):
             to = to_chip * 2 + i
-            staged[s, i] = total[i * dets : (i + 1) * dets].astype(BF16)
-            copy = det_send(staged.at[s, i], y_ref.at[chip], ys0.at[s, i], ys1.at[chip], to)
-
-            @pl.when(to != me)
+            staged[c, s, i] = total[i * chunk : (i + 1) * chunk].astype(BF16)
+            copy = det_send(
+                staged.at[c, s, i], y_ref.at[chip, cuts[c]], ys0.at[c, s, i], ys1.at[chip, c], to
+            )
+            direct = to != me
+            if relayed and c == 0 and s == 0:
+                direct = direct & mine
+                around = det_send(
+                    staged.at[c, s, i], by_y, vy0.at[i], vy1.at[0], back_chip * 2 + i
+                )
+
+                @pl.when(jnp.logical_not(mine))
+                def _():
+                    around.start()
+
+                sends.append((jnp.logical_not(mine), around))
+
+            @pl.when(direct)
             def _():
                 copy.start()
 
             @pl.when(to == me)
             def _():
-                y_ref[chip] = staged[s, i]
-
-            sends.append((to, copy))
+                y_ref[chip, cuts[c]] = staged[c, s, i]
+
+            sends.append((direct, copy))
 
     before = None
-    for s in range(hn):
-        near = lax.rem(chip + s, hn)
-        given[s] = product((1 - core) * hn + near).astype(BF16)
-        swaps.append(det_send(given.at[s], taken.at[s], ps0.at[s], ps1.at[s], partner))
-        swaps[-1].start()
-        total = product(core * hn + near)
-        if before is not None:
-            finish(s - 1, before)
-        before = total
-    finish(hn - 1, before)
+    for c in range(2):
+        for s in range(hn):
+            near = lax.rem(chip + s, hn)
+            given[c, s] = product((1 - core) * hn + near, c).astype(BF16)
+            swaps.append(
+                det_send(given.at[c, s], taken.at[c, s], ps0.at[c, s], ps1.at[c, s], partner)
+            )
+            swaps[-1].start()
+            total = product(core * hn + near, c)
+            if before is not None:
+                finish(*before)
+            before = (c, s, total)
+    finish(*before)
+    y_onward = det_send(
+        by_y, y_ref.at[from_chip, cuts[0]], wy0.at[0], ys1.at[from_chip, 0], final_chip * 2 + core
+    )
+    if relayed:
+        det_send(by_y, by_y, vy0.at[0], vy1.at[0], me).wait_recv()
+        y_onward.start()
+
     give_wait()
     wide[...] = gathered[...].reshape(obs * 64, LANES).astype(F32)
     prod = jnp.zeros((obs * 4, width), F32)
@@ -564,61 +636,61 @@
         finals[-1].start()
     eb_ref[me] = zz[pl.ds(me * per, per)]
 
-    for c in range(n):
-
-        @pl.when(c * 2 + side != me)
-        def _():
-            det_send(y_ref.at[c], y_ref.at[c], ys0.at[0, 0], ys1.at[c], me).wait_recv()
-
     for copy in finals:
         copy.wait()
-
-    def first(g, carry):
-        at = pl.ds(pl.multiple_of(g * 16, 16), 16)
-        re, im = [], []
-        for b in range(slow):
-            chip, lo = place(bands, b)
-            re.append(y_ref[chip, at, lo : lo + LANES].astype(F32))
-            im.append(y_ref[chip, at, lo + LANES : lo + FAST].astype(F32))
-        re, im = small_dft(re, im, 1)
-        for z in range(slow):
-            c, s = tw_ref[z, 0:1, :], tw_ref[z, 1:2, :]
-            turned[z, at, :LANES] = (re[z] * c - im[z] * s).astype(BF16)
-            turned[z, at, LANES:] = (im[z] * c + re[z] * s).astype(BF16)
-        return carry
-
-    lax.fori_loop(0, dets // 16, first, 0)
     for q in range(2):
         rows = eb_ref[:, q].reshape(8 * slow, LANES)
         esums[q] = split_dot(edge_ref[...], rows, COLS_COLS).astype(BF16).astype(F32)
 
-    def fast(z, carry):
-        o = jnp.dot(turned[z], inv_ref[...], preferred_element_type=F32)
-        at = pl.ds(pl.multiple_of(z * 8, 8), 8)
-        edge = [
-            lax.dot_general(
-                esums[q, at, :].astype(BF16), ends_ref[...], COLS_COLS, preferred_element_type=F32
-            )[: dets // 2]
-            for q in range(2)
-        ]
-        o = o + jnp.concatenate(edge, 0)
-        ts[z] = o[:, :LANES]
-        ts[slow + z] = o[:, LANES:]
-        return carry
-
-    lax.fori_loop(0, slow, fast, 0)
-
-    for h in range(2):
-
-        def swap(g, carry):
-            at = pl.ds(pl.multiple_of(g * 16, 16), 16)
-            out = digit_swap([ts[h * slow + z, at, :] for z in range(slow)])
-            for i in range(slow):
-                ts[h * slow + i, at, :] = out[i]
+    def inverse(c):
+        for i in range(n):
+
+            @pl.when(i * 2 + side != me)
+            def _():
+                det_send(
+                    y_ref.at[i, cuts[c]], y_ref.at[i, cuts[c]], ys0.at[0, 0, 0], ys1.at[i, c], me
+                ).wait_recv()
+
+        def first(g, carry):
+            at = pl.ds(pl.multiple_of(c * chunk + g * 16, 16), 16)
+            re, im = [], []
+            for b in range(slow):
+                to, lo = place(bands, b)
+                re.append(y_ref[to, at, lo : lo + LANES].astype(F32))
+                im.append(y_ref[to, at, lo + LANES : lo + FAST].astype(F32))
+            re, im = small_dft(re, im, 1)
+            for z in range(slow):
+                cs, sn = tw_ref[z, 0:1, :], tw_ref[z, 1:2, :]
+                turned[z, at, :LANES] = (re[z] * cs - im[z] * sn).astype(BF16)
+                turned[z, at, LANES:] = (im[z] * cs + re[z] * sn).astype(BF16)
             return carry
 
-        lax.fori_loop(0, dets // 16, swap, 0)
-
+        lax.fori_loop(0, chunk // 16, first, 0)
+
+        def fast(z, carry):
+            at = pl.ds(pl.multiple_of(z * 8, 8), 8)
+            o = jnp.dot(turned[z, cuts[c]], inv_ref[...], preferred_element_type=F32)
+            o = o + lax.dot_general(
+                esums[c, at, :].astype(BF16), ends_ref[...], COLS_COLS, preferred_element_type=F32
+            )[:chunk]
+            ts[z, cuts[c]] = o[:, :LANES]
+            ts[slow + z, cuts[c]] = o[:, LANES:]
+            return carry
+
+        lax.fori_loop(0, slow, fast, 0)
+        for h in range(2):
+
+            def swap(g, carry):
+                at = pl.ds(pl.multiple_of(c * chunk + g * 16, 16), 16)
+                out = digit_swap([ts[h * slow + z, at, :] for z in range(slow)])
+                for i in range(slow):
+                    ts[h * slow + i, at, :] = out[i]
+                return carry
+
+            lax.fori_loop(0, chunk // 16, swap, 0)
+
+    inverse(0)
+    inverse(1)
     for i in range(tiles // 4):
         filtered = [
             (ts[k] * w_ref[:, k * LANES : (k + 1) * LANES].astype(F32)).astype(BF16)
@@ -666,18 +738,28 @@
         sky_ref[4 * i : 4 * i + 4] = got.reshape(4, rows_all, LANES)
     for copy in swaps:
         copy.wait_send()
-    for to, copy in sends:
-
-        @pl.when(to != me)
+    for started, copy in sends:
+
+        @pl.when(started)
         def _():
             copy.wait_send()
 
-    for d in far_first(n)[:-1]:
-        column(d).wait_send()
+    for copy in lefts:
+        copy.wait_send()
 
     @pl.when(jnp.logical_not(mine))
     def _():
-        column(0).wait_send()
+        for c in range(2):
+            column(0, c).wait_send()
+
+    if relayed:
+        over(0).wait_send()
+        y_onward.wait_send()
+
+        @pl.when(core == from_side)
+        def _():
+            for source in range(2):
+                onward(source).wait_send()
 
     for d in range(1, across):
         sideways(d).wait_send()
@@ -744,7 +826,7 @@
     row_buffer = pltpu.VMEM((tiles * MP, LANES), F32)
     pieces = pltpu.VMEM((n, tiles * MP, LANES), BF16)
     edge_rows = pltpu.VMEM((8 * det, LANES), F32)
-    mixed = pltpu.VMEM((half, 2 * dets, 2 * FAST), BF16)
+    mixed = pltpu.VMEM((2, half, dets, 2 * FAST), BF16)
     normal = call(
         functools.partial(normal_kernel, obs, det, grid),
         jax.ShapeDtypeStruct((held, rows_all, LANES), F32),
@@ -775,7 +857,7 @@
             pltpu.VMEM(member.shape, BF16),
             mixed,
             mixed,
-            pltpu.VMEM((half, 2, dets, 2 * FAST), BF16),
+            pltpu.VMEM((2, half, 2, dets // 2, 2 * FAST), BF16),
             pltpu.VMEM(member.shape, BF16),
             pltpu.VMEM((det, per, CAP * MP, LANES), F32),
             pltpu.VMEM((det, dets, FAST), BF16),
@@ -789,17 +871,22 @@
             slot_buffer,
             slot_buffer,
             pltpu.VMEM((det, held * MP, LANES), BF16),
+            pltpu.VMEM((2, dets // 2, 2 * FAST), BF16),
+            pltpu.VMEM((dets // 2, 2 * FAST), BF16),
             *dma(obs),
             *dma(2),
             *dma(grid[0]),
             *[pltpu.SemaphoreType.DMA((2, down // 2))] * 2,
-            *dma(n),
+            *[pltpu.SemaphoreType.DMA((n, 2))] * 2,
             *dma(det),
             *dma(obs),
             *dma(obs),
-            *dma(half),
-            pltpu.SemaphoreType.DMA((half, 2)),
-            pltpu.SemaphoreType.DMA((n,)),
+            *[pltpu.SemaphoreType.DMA((2, half))] * 2,
+            pltpu.SemaphoreType.DMA((2, half, 2)),
+            pltpu.SemaphoreType.DMA((n, 2)),
+            *dma(2),
+            *dma(2),
+            *dma(1),
             *dma(det),
             *dma(1),
             *dma(n),

time: 142 us -> 138 us (0.972)
  Pallas kernels: 139 us -> 135 us
    pallas_call x1, Pallas kernels: 139 us -> 135 us  [run(): pl.pallas_call(kernel, out_shape=out, in_specs=[VMEM] * len(args), out_sp...]
where the time goes in v5:
time: 138 us
  Pallas kernels  135 us (98%)
  local copies, waits for them, and re-layouts  3.47 us (3%)
    pallas_call x1, Pallas kernels, run(): pl.pallas_call(kernel, out_shape=out, in_specs=[VMEM] * len(args), out_sp...  135 us
    unnamed x2, local copies, waits for them, and re-layouts  3.47 us

profile of v5, /device:TPU:1, one launch (start us, length us, event | category | flops | bytes accessed | tf_op | source)
XLA Modules:
  0.0 138.2 jit_solution(12836177930133756391)
XLA Ops:
  0.0 1.4 %copy.14.kernel_ref = bf16[96,48]{1,0:T(8,128)(2,1)} copy(bf16[96,48]{0,1:T(8,128)(2,1)} %param.16) | data formatting | bytes 18432 | tf_op args[3]
  1.4 134.7 %normal.1 = f32[32,48,128]{2,1,0:T(8,128)} custom-call(bf16[1536,128]{1,0:T(8,128)(2,1)} %bitcast.6, s32[32,32]{1,0:T(8,128)} %list_ref.1, bf16[32,128,128]{2,1,0:T(8,128)(2,1)} %bitcast.5, bf16[48,1536]{1,0:T(8,128)(2,1)} %bitcast.7, bf16[96,48]{1,0:T(8,128)(2,1)} %copy.14.kernel_ref, bf16[96,4096]{1,0:T(8,128)(2,1)} %w_ref.1, ...), custom_call_target="tpu_custom_call" | custom-call | tf_op jit(solution)/shard_map/normal/pallas_call | solution.py:780
  136.2 2.1 %copy.16 = f32[32,3,16,128]{3,2,1,0:T(8,128)} copy(f32[32,3,16,128]{3,2,1,0:T(8,128)} %bitcast.4) | data formatting | bytes 1572864

commit v6 on v5

--- a/solution.py
+++ b/solution.py
@@ -190,7 +190,9 @@
         )
 
     n = det // 2
-    order = sorted(range(1, n), key=lambda d: -min(d, n - d))
+    far = n // 2
+    handed = n >= 4
+    order = [d for d in far_first(n)[:-1] if d != far or not handed]
     outs = []
     for d in order:
         outs.append(copy(me, others[d - 1], send_sem.at[d], recv_sem.at[d]))
@@ -198,9 +200,12 @@
     outs.append(copy(me, partner, pass_send.at[0], pass_recv.at[0]))
     outs[-1].start()
     sent()
-    for d in reversed(order):
+    for d in order[::-1] + ([far] if handed else []):
         source = lax.rem(me + det - 2 * d, det)
         copy(source, me, send_sem.at[d], recv_sem.at[d]).wait_recv()
+        if handed and d == n - far + 1:
+            outs.append(copy(source, others[n - 2], send_sem.at[far], recv_sem.at[far]))
+            outs[-1].start()
         outs.append(copy(source, partner, pass_send.at[d], pass_recv.at[d]))
         outs[-1].start()
     for d in range(n):
@@ -391,8 +396,8 @@
 
     for q in range(4):
         cut = expand_ref[:, q * det * 16 : (q + 1) * det * 16]
-        ke_ref[q * dets : (q + 1) * dets] = jnp.dot(
-            kernel_ref[...], cut, preferred_element_type=F32
+        ke_ref[q * dets : (q + 1) * dets] = lax.dot_general(
+            kernel_ref[...], cut, COLS_COLS, preferred_element_type=F32
         ).astype(BF16)
 
     sky_wait()
@@ -497,11 +502,12 @@
         def _():
             column(0, c).start()
 
+    advance()
     timestream(0)
     transform(0)
     send_columns(0)
+    timestream(1)
     advance()
-    timestream(1)
 
     sums[...] = jnp.zeros_like(sums)
 
@@ -513,7 +519,6 @@
 
     transform(1)
     send_columns(1)
-    advance()
     if relayed:
 
         @pl.when(core == from_side)
@@ -539,8 +544,9 @@
     for i in range(4):
         payload[16 * i : 16 * i + det] = es[pl.ds(i, det, stride=8), :].astype(BF16)
     give_start, give_wait = obs_copies(obs, payload, gathered, gs0, gs1, True)
+    for step in steps:
+        turn(step)
     give_start()
-    advance()
     for i in range(n):
 
         @pl.when(core * n + i != me)
@@ -549,9 +555,6 @@
                 det_send(
                     x_out.at[i, cuts[c]], x_out.at[i, cuts[c]], xs0.at[0, c], xs1.at[i, c], me
                 ).wait_recv()
-
-    for step in steps:
-        turn(step)
 
     hn = n // 2
     swaps, sends = [], []
@@ -899,7 +902,7 @@
         "normal",
         0,
     )(
-        sky.reshape(held * rows_all, LANES), tile_list, block, noise_inverse[0], detector_kernel, sample_weight,
+        sky.reshape(held * rows_all, LANES), tile_list, block, noise_inverse[0], detector_kernel.T, sample_weight,
         expand, fwd, inv, tw, edge, ends, sel,
     )
     return normal.reshape(sky.shape)

time: 138 us -> 140 us (1.014)
  Pallas kernels: 135 us -> 138 us
  local copies, waits for them, and re-layouts: 3.47 us -> 2.06 us
    pallas_call x1, Pallas kernels: 135 us -> 138 us  [run(): pl.pallas_call(kernel, out_shape=out, in_specs=[VMEM] * len(args), out_sp...]
    unnamed x2 -> x1, local copies, waits for them, and re-layouts: 3.47 us -> 2.06 us
where the time goes in v6:
time: 140 us
  Pallas kernels  138 us (99%)
  local copies, waits for them, and re-layouts  2.06 us (1%)
    pallas_call x1, Pallas kernels, run(): pl.pallas_call(kernel, out_shape=out, in_specs=[VMEM] * len(args), out_sp...  138 us

profile of v6, /device:TPU:1, one launch (start us, length us, event | category | flops | bytes accessed | tf_op | source)
XLA Modules:
  0.0 139.8 jit_solution(7449415276504394496)
XLA Ops:
  0.0 137.7 %normal.1 = f32[32,48,128]{2,1,0:T(8,128)} custom-call(bf16[1536,128]{1,0:T(8,128)(2,1)} %bitcast.7, s32[32,32]{1,0:T(8,128)} %list_ref.1, bf16[32,128,128]{2,1,0:T(8,128)(2,1)} %bitcast.6, bf16[48,1536]{1,0:T(8,128)(2,1)} %bitcast.8, bf16[48,96]{1,0:T(8,128)(2,1)} %bitcast.9, bf16[96,4096]{1,0:T(8,128)(2,1)} %w_ref.1, ...), custom_call_target="tpu_custom_call" | custom-call | tf_op jit(solution)/shard_map/normal/pallas_call | solution.py:783
  137.7 2.1 %copy.15 = f32[32,3,16,128]{3,2,1,0:T(8,128)} copy(f32[32,3,16,128]{3,2,1,0:T(8,128)} %bitcast.5) | data formatting | bytes 1572864

commit v7 on v6

--- a/solution.py
+++ b/solution.py
@@ -559,8 +559,8 @@
     hn = n // 2
     swaps, sends = [], []
 
-    def product(to_chip, c):
-        blocks = [to_chip * 4 + 2 * i + c for i in range(2)]
+    def product(to_chips, c):
+        blocks = [to_chip * 4 + 2 * i + c for to_chip in to_chips for i in range(2)]
         rows = jnp.concatenate([m_out[at // down, lax.rem(at, down)] for at in blocks], 0)
         return jnp.dot(rows, x_out[...].reshape(n * dets, 2 * FAST), preferred_element_type=F32)
 
@@ -601,12 +601,13 @@
     for c in range(2):
         for s in range(hn):
             near = lax.rem(chip + s, hn)
-            given[c, s] = product((1 - core) * hn + near, c).astype(BF16)
+            got = product(((1 - core) * hn + near, core * hn + near), c)
+            given[c, s] = got[:dets].astype(BF16)
             swaps.append(
                 det_send(given.at[c, s], taken.at[c, s], ps0.at[c, s], ps1.at[c, s], partner)
             )
             swaps[-1].start()
-            total = product(core * hn + near, c)
+            total = got[dets:]
             if before is not None:
                 finish(*before)
             before = (c, s, total)

time: 140 us -> 140 us (level)
  no operation moved by 1% of the time
where the time goes in v7:
time: 140 us
  Pallas kernels  138 us (99%)
  local copies, waits for them, and re-layouts  2.06 us (1%)
    pallas_call x1, Pallas kernels, run(): pl.pallas_call(kernel, out_shape=out, in_specs=[VMEM] * len(args), out_sp...  138 us

profile of v7, /device:TPU:1, one launch (start us, length us, event | category | flops | bytes accessed | tf_op | source)
XLA Modules:
  0.0 139.9 jit_solution(17448689025648484351)
XLA Ops:
  0.0 137.8 %normal.1 = f32[32,48,128]{2,1,0:T(8,128)} custom-call(bf16[1536,128]{1,0:T(8,128)(2,1)} %bitcast.7, s32[32,32]{1,0:T(8,128)} %list_ref.1, bf16[32,128,128]{2,1,0:T(8,128)(2,1)} %bitcast.6, bf16[48,1536]{1,0:T(8,128)(2,1)} %bitcast.8, bf16[48,96]{1,0:T(8,128)(2,1)} %bitcast.9, bf16[96,4096]{1,0:T(8,128)(2,1)} %w_ref.1, ...), custom_call_target="tpu_custom_call" | custom-call | tf_op jit(solution)/shard_map/normal/pallas_call | solution.py:784
  137.9 2.1 %copy.15 = f32[32,3,16,128]{3,2,1,0:T(8,128)} copy(f32[32,3,16,128]{3,2,1,0:T(8,128)} %bitcast.5) | data formatting | bytes 1572864
